TPU v7x, 512 devices: a whole 4x8x8 slice. The times are simulated.
512 devices in a mesh: row: 16 (over y, x_hi), col: 32 (over z, x_lo, core).
Axes of the slice: x: 4 (x_hi: 2, x_lo: 2; x = x_hi * 2 + x_lo), y: 8, z: 8, core: 2. Of those that a mesh axis runs over, the one named last changes fastest.
Arguments:
- features: bfloat16 [32, 2048, 128], P('col'), may hold values from -6 to 6
- dst_features: bfloat16 [65536, 128], P(('row', 'col')), may hold values from -6 to 6
- w_self: bfloat16 [128, 256], replicated, may hold values from -0.5 to 0.5
- w_neigh: bfloat16 [128, 256], replicated, may hold values from -0.5 to 0.5
- cotangent: bfloat16 [65536, 256], P(('row', 'col')), may hold values from -6 to 6
- block_values: bfloat16 [16, 32, 32, 128, 128], P('row', 'col'), may hold values from -0.15625 to 0.15625
- block_rows: int32 [16, 32, 32], P('row', 'col'), may hold values from 0 to 31, as said below
- block_cols: int32 [16, 32, 32], P('row', 'col'), may hold values from 0 to 15
- block_counts: int32 [16, 32], P('row', 'col'), may hold values from 4 to 32, as said below
Outputs:
- output: bfloat16 [65536, 256], P(('row', 'col'))
- grad_w_self: float32 [128, 256], replicated
- grad_w_neigh: float32 [128, 256], replicated
- grad_features: float32 [32, 2048, 128], P('col', 'row')
Inputs may be any that keep to these rules, and one draw needn't show every extreme that they name: On one device the slots name distinct pairs of block_rows and block_cols, also in unused slots. `block_counts`: some device uses all 32 slots in every draw.
All inputs are finite; a program needn't handle non-finite values.
Results may differ from a plain program's by a relative error of at most 0.0052.
Values may be sent and summed in bfloat16 or wider, within the bound.
A program may use at most 64 MiB of HBM per device.

v0:
```python
import math

import jax
import jax.numpy as jnp
from jax import lax
from jax.sharding import PartitionSpec as P


def slot_products(block_vals, source_table, slot_index, einsum_form):
    return jnp.einsum(
        einsum_form, block_vals, source_table[slot_index], preferred_element_type=jnp.float32
    )


def per_device(
    features,
    dst_features,
    w_self,
    w_neigh,
    cotangent,
    block_values,
    block_rows,
    block_cols,
    block_counts,
):
    block_size = block_values.shape[-1]
    feat_width = features.shape[-1]
    local_rows = dst_features.shape[0]
    col_total = lax.axis_size("col")
    slab_blocks = local_rows * col_total // block_size
    source_table = features.reshape(-1, block_size, feat_width)
    source_count = source_table.shape[0]
    block_vals = block_values[0, 0]
    row_ids = block_rows[0, 0]
    col_ids = block_cols[0, 0]
    live_count = block_counts[0, 0]
    slot_total = row_ids.shape[0]
    live_mask = jnp.arange(slot_total, dtype=jnp.int32) < live_count
    row_hits = (
        (row_ids[None, :] == jnp.arange(slab_blocks, dtype=jnp.int32)[:, None]) & live_mask[None, :]
    ).astype(jnp.float32)
    forward_terms = slot_products(block_vals, source_table, col_ids, "sij,sjf->sif")
    summed = jnp.einsum("rs,sif->rif", row_hits, forward_terms, precision=lax.Precision.HIGHEST)
    agg_sum = lax.psum_scatter(
        summed.reshape(local_rows * lax.axis_size("col"), feat_width),
        "col",
        scatter_dimension=0,
        tiled=True,
    )
    aggregate = agg_sum.astype(jnp.bfloat16)
    pre_act = jnp.dot(dst_features, w_self, preferred_element_type=jnp.float32) + jnp.dot(
        aggregate, w_neigh, preferred_element_type=jnp.float32
    )
    sigmoid_pre = jax.nn.sigmoid(pre_act)
    output = (pre_act * sigmoid_pre).astype(jnp.bfloat16)
    grad_pre = (
        cotangent.astype(jnp.float32) * sigmoid_pre * (1.0 + pre_act * (1.0 - sigmoid_pre))
    ).astype(jnp.bfloat16)
    node_total = local_rows * lax.axis_size("row") * col_total
    scale_factor = 1.0 / math.sqrt(node_total)
    self_grad = jnp.einsum("nf,nh->fh", dst_features, grad_pre, preferred_element_type=jnp.float32)
    neigh_grad = jnp.einsum("nf,nh->fh", aggregate, grad_pre, preferred_element_type=jnp.float32)
    self_sum, neigh_sum = lax.psum((self_grad, neigh_grad), ("row", "col"))
    local_grad = jnp.einsum(
        "nh,fh->nf", grad_pre, w_neigh, preferred_element_type=jnp.float32
    ).astype(jnp.bfloat16)
    slab_grad = lax.all_gather(local_grad, "col", axis=0, tiled=True)
    grad_table = slab_grad.reshape(slab_blocks, block_size, feat_width)
    backward_terms = slot_products(block_vals, grad_table, row_ids, "sij,sif->sjf")
    col_hits = (
        (col_ids[None, :] == jnp.arange(source_count, dtype=jnp.int32)[:, None])
        & live_mask[None, :]
    ).astype(jnp.float32)
    source_terms = jnp.einsum(
        "cs,sjf->cjf", col_hits, backward_terms, precision=lax.Precision.HIGHEST
    ).reshape(-1, feat_width)
    source_part = lax.psum_scatter(source_terms, "row", scatter_dimension=0, tiled=True)
    return (
        output,
        self_sum * scale_factor,
        neigh_sum * scale_factor,
        source_part.reshape(1, -1, feat_width),
    )


def solution(mesh):
    placed = (
        P("col", None, None),
        P(("row", "col"), None),
        P(),
        P(),
        P(("row", "col"), None),
        P("row", "col", None, None, None),
        P("row", "col", None),
        P("row", "col", None),
        P("row", "col"),
    )
    return jax.shard_map(
        per_device,
        mesh=mesh,
        in_specs=placed,
        out_specs=(P(("row", "col"), None), P(), P(), P("col", "row", None)),
        check_vma=False,
    )
```

profile of v0, /device:TPU:1, one launch (start us, length us, event | category | flops | bytes accessed | tf_op | source)
XLA Modules:
  0.0 697.7 jit_solution(4395809418823105912)
XLA Ops:
  7.2 0.0 copy-start
  7.2 0.0 reduce-scatter.3.cloned.1.call-start
  8.0 0.7 fusion.21
  8.6 1.8 gather_fusion
  10.4 0.0 copy-done
  10.4 2.2 fusion.6
  12.7 0.0 copy-start.4
  12.7 2.4 copy.21
  15.1 0.0 copy-done.4
  15.1 1.1 fusion.2
  16.2 2.6 copy.16
  18.8 0.0 copy-start.1
  18.8 0.0 copy-start.2
  18.8 0.0 copy-start.3
  18.8 0.0 copy-start.6
  18.8 0.0 reduce-scatter.3.cloned.1.call-update
  18.8 0.0 all-gather.2.cloned.1.call-start
  18.8 0.7 copy-done.1
  19.5 0.1 copy-done.2
  19.6 0.1 fusion.23
  19.8 123.1 %reduce-scatter.3.cloned.1.call-done = f32[128,128]{1,0:T(8,128)} async-done(((f32[4096,128]{1,0:T(8,128)}), f32[128,128]{1,0:T(8,128)}) %reduce-scatter.3.cloned.1.call-update) | async-done | bytes 65552 | tf_op jit(solution)/shard_map/reduce_scatter | solution.py:44
  142.9 0.0 copy-done.3
  142.9 0.0 copy-done.6
  142.9 1.7 multiply_convert_fusion
  144.6 0.8 convolution_convert_fusion
  145.4 0.0 all-gather.2.cloned.1.call-update
  145.4 0.0 all-reduce.3.cloned.1.call-start
  145.5 0.8 convolution_bitcast_fusion
  146.3 1.7 fusion.8
  148.0 0.0 all-reduce.3.cloned.1.call-update
  148.0 0.0 reduce-scatter.5.cloned.1.call-start
  148.1 65.6 %all-gather.2.cloned.1.call-done = bf16[4096,128]{1,0:T(8,128)(2,1)} async-done(((bf16[128,128]{1,0:T(8,128)(2,1)}), bf16[4096,128]{1,0:T(8,128)(2,1)}) %all-gather.2.cloned.1.call-update) | async-done | bytes 1048592 | tf_op jit(solution)/shard_map/all_gather | solution.py:67
  213.7 2.0 gather_fusion.1
  215.7 1.9 fusion.4
  217.6 0.0 copy-start.5
  217.6 2.4 copy.23
  220.0 0.0 copy-done.5
  220.0 0.8 fusion
  220.8 1.3 copy.18
  222.1 0.0 reduce-scatter.5.cloned.1.call-update
  222.1 265.1 %all-reduce.3.cloned.1.call-done = (f32[128,256]{0,1:T(8,128)}, f32[128,256]{0,1:T(8,128)}) async-done(((f32[128,256]{0,1:T(8,128)}, f32[128,256]{0,1:T(8,128)}), (f32[128,256]{0,1:T(8,128)}, f32[128,256]{0,1:T(8,128)})) %all-reduce.3.cloned.1.call-update) | async-done | bytes 262160 | tf_op jit(solution)/shard_map/psum | solution.py:63
  487.2 1.0 broadcast_multiply_fusion
  488.2 0.8 copy.20
  489.0 0.8 copy.19
  489.7 201.4 %reduce-scatter.5.cloned.1.call-done = f32[128,128]{1,0:T(8,128)} async-done(((f32[2048,128]{1,0:T(8,128)}), f32[128,128]{1,0:T(8,128)}) %reduce-scatter.5.cloned.1.call-update) | async-done | bytes 65552 | tf_op jit(solution)/shard_map/reduce_scatter | solution.py:77
  (4 shorter events, 0.0 us)
Async XLA Ops:
  7.2 3.3 copy-start
  7.2 135.7 %reduce-scatter.3.cloned.1.call-start = ((), (), s32[]{:S(2)}) async-start(), calls=%async_computation.2 | async-start | bytes 2162688 | tf_op jit(solution)/shard_map/reduce_scatter | solution.py:44
  12.7 2.4 copy-start.4
  18.8 0.8 copy-start.1
  18.8 0.9 copy-start.2
  18.8 124.1 %copy-start.3 = (bf16[128,256]{1,0:T(8,128)(2,1)S(1)}, bf16[128,256]{1,0:T(8,128)(2,1)}, u32[]{:S(2)}) copy-start(bf16[128,256]{1,0:T(8,128)(2,1)} %param.12) | copy-start | bytes 196612
  18.8 124.1 %copy-start.6 = (bf16[128,256]{1,0:T(8,128)(2,1)S(1)}, bf16[128,256]{1,0:T(8,128)(2,1)}, u32[]{:S(2)}) copy-start(bf16[128,256]{1,0:T(8,128)(2,1)} %param.13) | copy-start | bytes 196612
  18.8 194.9 %all-gather.2.cloned.1.call-start = ((), (), s32[]{:S(2)}) async-start(), calls=%async_computation.3 | async-start | bytes 1081344 | tf_op jit(solution)/shard_map/all_gather | solution.py:67
  145.4 341.9 %all-reduce.3.cloned.1.call-start = ((), (), s32[]{:S(2)}) async-start(), calls=%async_computation.5 | async-start | bytes 524288 | tf_op jit(solution)/shard_map/psum | solution.py:63
  148.0 543.1 %reduce-scatter.5.cloned.1.call-start = ((), (), s32[]{:S(2)}) async-start(), calls=%async_computation.4 | async-start | bytes 1114112 | tf_op jit(solution)/shard_map/reduce_scatter | solution.py:77
  217.6 2.4 copy-start.5
Sparse Core Ops, SparseCore 0:
  18.9 123.9 reduce-scatter.2
  145.8 67.8 all-gather.1
  220.3 266.8 all-reduce.2
  492.1 199.0 reduce-scatter.4
where the time goes:
time: 702 us; the launch traced here: 698 us
  waiting for transfers between devices  655 us (93%)
  local copies, waits for them, and re-layouts  14.7 us (2%)
  between operations  14.6 us (2%)
  matrix products  11.2 us (2%)
    psum x1, waiting for transfers between devices, per_device(): self_sum, neigh_sum = lax.psum((self_grad, neigh_grad), ('row', 'col'))  265 us
    reduce_scatter x1, waiting for transfers between devices, per_device(): lax.psum_scatter(source_terms, 'row', scatter_dimension=0, tiled=True)  201 us
    reduce_scatter x1, waiting for transfers between devices, per_device(): lax.psum_scatter(summed.reshape(local_rows * lax.axis_size('col'), feat_w...  123 us
    all_gather x1, waiting for transfers between devices, per_device(): slab_grad = lax.all_gather(local_grad, 'col', axis=0, tiled=True)  65.6 us
  transfers between devices with their start and end apart: 4, of which 4 were waited for; matrix products, arithmetic and copies ran while one was open for 2% of the time, Pallas kernels for 0%

commit v1 on v0

v1 whole, which is shorter than its diff:
```python
import functools
import math

import jax
import jax.numpy as jnp
from jax import lax
from jax.experimental import pallas as pl
from jax.experimental.pallas import tpu as pltpu
from jax.sharding import PartitionSpec as P

BF16 = jnp.bfloat16
F32 = jnp.float32
MESH = pl.DeviceIdType.MESH
N = 8
VMEM = pl.BlockSpec(memory_space=pltpu.VMEM)
SMEM = pl.BlockSpec(memory_space=pltpu.SMEM)
LIMIT = 32 * 1024 * 1024


def near(i):
    hop = i // 2 + 1
    return hop + (i % 2) * (N - 2 * hop)


def far(i):
    return near(N - 2 - i)


def loop(n, body):
    lax.fori_loop(0, n, lambda i, c: (body(i), c)[1], 0)


def remote(src, dst, send, recv, device):
    return pltpu.make_async_remote_copy(
        src_ref=src, dst_ref=dst, send_sem=send, recv_sem=recv, device_id=device, device_id_type=MESH
    )


def col_parts():
    c = lax.axis_index("col")
    return c // 4, (c // 2) % 2, c % 2


def row_parts():
    r = lax.axis_index("row")
    return r // 2, r % 2


def forward_kernel(rows, cols, counts, feats, vals, send, keep, acc):
    core = lax.axis_index("col") % 2
    slots = vals.shape[0]
    live = counts[0, 0]
    half = keep.shape[0]
    acc[...] = jnp.zeros_like(acc)
    for s in range(slots):
        r = rows[0, 0, s]
        at = ((r + core) % 2) * half + ((r // 2) % 2) * N + r // 4
        at = jnp.where(s < live, at, 2 * half)
        acc[at] += jnp.dot(vals[s], feats[cols[0, 0, s]], preferred_element_type=F32)
    keep[...] = acc[:half]
    send[...] = acc[half : 2 * half].astype(BF16)


def backward_kernel(rows, cols, counts, grads, vals, send, keep, acc):
    side = lax.axis_index("row") % 2
    slots = vals.shape[0]
    live = counts[0, 0]
    half = keep.shape[0]
    acc[...] = jnp.zeros_like(acc)
    for s in range(slots):
        r = rows[0, 0, s]
        c = cols[0, 0, s]
        at = ((c + side) % 2) * half + c // 2
        at = jnp.where(s < live, at, 2 * half)
        g = grads[(r % 2) * 16 + ((r // 2) % 2) * N + r // 4]
        acc[at] += lax.dot_general(vals[s], g, (((0,), (0,)), ((), ())), preferred_element_type=F32)
    keep[...] = acc[:half]
    send[...] = acc[half : 2 * half].astype(BF16)


def products(kernel, half, rows, cols, counts, table, vals):
    block, width = vals.shape[-1], table.shape[-1]
    slots = vals.shape[0]
    return pl.pallas_call(
        kernel,
        out_shape=(
            jax.ShapeDtypeStruct((half, block, width), BF16),
            jax.ShapeDtypeStruct((half, block, width), F32),
        ),
        in_specs=[SMEM, SMEM, SMEM, VMEM, VMEM],
        out_specs=(VMEM, VMEM),
        scratch_shapes=[pltpu.VMEM((2 * half + 1, block, width), F32)],
        compiler_params=pltpu.CompilerParams(vmem_limit_bytes=LIMIT),
        cost_estimate=pl.CostEstimate(
            flops=2 * slots * block * block * width,
            bytes_accessed=2 * slots * block * block + 6 * half * block * width,
            transcendentals=0,
        ),
    )(rows, cols, counts, table, vals)


def dense_kernel(
    psend, pkeep, dst, cot, w_self, w_neigh,
    out, grads, wpart,
    got_c, x_send, got_x, z_send, got_z, own,
    w_full, w_c, w_xs, w_x, w_zs, w_z,
    c_s, c_r, x_s, x_r, z_s, z_r,
    gz_s, gz_r, gx_s, gx_r, gc_s, gc_r,
    wc_s, wc_r, wx_s, wx_r, wz_s, wz_r,
):
    row = lax.axis_index("row")
    z, x, k = col_parts()
    sibling = (row, z * 4 + x * 2 + (1 - k))
    beside = (row, z * 4 + (1 - x) * 2 + k)

    def ring(d):
        other = (z + d) % N
        return other, (row, other * 4 + x * 2 + k)

    barrier = pltpu.get_barrier_semaphore()
    pl.semaphore_signal(barrier, inc=1, device_id=sibling, device_id_type=MESH)
    pl.semaphore_signal(barrier, inc=1, device_id=beside, device_id_type=MESH)
    for d in range(1, N):
        pl.semaphore_signal(barrier, inc=1, device_id=ring(d)[1], device_id_type=MESH)
    pl.semaphore_wait(barrier, N + 1)

    def c_copy(at):
        return remote(psend.at[at], got_c.at[at], c_s.at[at], c_r.at[at], sibling)

    away, here = (1 - x) * N, x * N

    def c_start(i):
        c_copy(away + (z + far(i)) % N).start()

    def c_start_here(i):
        c_copy(here + (z + far(i)) % N).start()

    loop(N - 1, c_start)
    c_copy(away + z).start()
    loop(N - 1, c_start_here)
    c_copy(here + z).start()

    def x_copy(at):
        return remote(x_send.at[at], got_x.at[at], x_s.at[at], x_r.at[at], beside)

    def x_step(at):
        c_copy(away + at).wait_recv()
        x_send[at] = (pkeep[away + at] + got_c[away + at].astype(F32)).astype(BF16)
        x_copy(at).start()

    loop(N - 1, lambda i: x_step((z + far(i)) % N))
    x_step(z)

    pre_self = jnp.dot(dst[...], w_self[...], preferred_element_type=F32)

    def z_copy(d):
        other, device = ring(d)
        return remote(z_send.at[other], got_z.at[z], z_s.at[d], z_r.at[d], device)

    def merged(at):
        c_copy(here + at).wait_recv()
        x_copy(at).wait_recv()
        return pkeep[here + at] + got_c[here + at].astype(F32) + got_x[at].astype(F32)

    def z_step(i):
        d = far(i)
        other = (z + d) % N
        z_send[other] = merged(other).astype(BF16)
        z_copy(d).start()

    loop(N - 1, z_step)
    own[...] = merged(z)

    def z_take(i):
        d = near(i)
        z_copy(d).wait_recv()
        own[...] += got_z[(z + N - d) % N].astype(F32)

    loop(N - 1, z_take)
    agg = own[...].astype(BF16)

    pre = pre_self + jnp.dot(agg, w_neigh[...], preferred_element_type=F32)
    sig = jax.nn.sigmoid(pre)
    out[...] = (pre * sig).astype(BF16)
    gpre = (cot[...].astype(F32) * sig * (1.0 + pre * (1.0 - sig))).astype(BF16)
    me = k * 16 + x * N + z
    grads[me] = lax.dot_general(
        gpre, w_neigh[...], (((1,), (1,)), ((), ())), preferred_element_type=F32
    ).astype(BF16)

    mine = k * 16 + x * N
    besides = k * 16 + (1 - x) * N

    def gz_copy(d):
        return remote(grads.at[me], grads.at[me], gz_s.at[d], gz_r.at[d], ring(d)[1])

    def gx_copy(at):
        return remote(grads.at[mine + at], grads.at[mine + at], gx_s.at[at], gx_r.at[at], beside)

    def gc_copy(part, at):
        slot = k * 16 + part * N + at
        sem = part * N + at
        return remote(grads.at[slot], grads.at[slot], gc_s.at[sem], gc_r.at[sem], sibling)

    loop(N - 1, lambda i: gz_copy(far(i)).start())
    gx_copy(z).start()
    gc_copy(x, z).start()

    feat = dst.shape[1]
    pieces, tall, hid = w_full.shape
    for base, left in ((0, dst[...]), (1, agg)):
        dw = lax.dot_general(left, gpre, (((0,), (0,)), ((), ())), preferred_element_type=F32)
        w_full[pl.ds(base * (feat // tall), feat // tall)] = dw.reshape(feat // tall, tall, hid)
    half = pieces // 2
    wc_copy = remote(w_full.at[pl.ds((1 - k) * half, half)], w_c, wc_s, wc_r, sibling)
    wc_copy.start()

    def forward(i):
        d = near(i)
        other = (z + N - d) % N
        gz_copy(d).wait_recv()
        gx_copy(other).start()
        gc_copy(x, other).start()

    lax.fori_loop(0, 2, lambda i, c: (forward(i), c)[1], 0)
    wc_copy.wait_recv()
    w_xs[...] = w_full[pl.ds(k * half + (1 - x) * N, N)] + w_c[pl.ds((1 - x) * N, N)]
    wx_copy = remote(w_xs, w_x, wx_s, wx_r, beside)
    wx_copy.start()
    lax.fori_loop(2, 4, lambda i, c: (forward(i), c)[1], 0)
    wx_copy.wait_recv()
    w_zs[...] = w_full[pl.ds(k * half + x * N, N)] + w_c[pl.ds(x * N, N)] + w_x[...]

    def wz_copy(d):
        other, device = ring(d)
        return remote(w_zs.at[other], w_z.at[z], wz_s.at[d], wz_r.at[d], device)

    loop(N - 1, lambda i: wz_copy(far(i)).start())
    lax.fori_loop(4, N - 1, lambda i, c: (forward(i), c)[1], 0)

    def gx_take(at):
        gx_copy(at).wait_recv()
        gc_copy(1 - x, at).start()

    gx_take(z)
    loop(N - 1, lambda i: gx_take((z + near(i)) % N))

    wpart[...] = w_zs[z]

    def wz_take(i):
        d = near(i)
        wz_copy(d).wait_recv()
        wpart[...] += w_z[(z + N - d) % N]

    loop(N - 1, wz_take)

    def gc_wait(i):
        gc_copy(i // N, i % N).wait_recv()

    loop(2 * N, gc_wait)

    loop(2 * N, lambda i: c_copy(i).wait_send())
    loop(N, lambda i: x_copy(i).wait_send())
    loop(N, lambda i: gx_copy(i).wait_send())
    loop(2 * N, lambda i: gc_copy(i // N, i % N).wait_send())

    def ring_sent(i):
        z_copy(i + 1).wait_send()
        gz_copy(i + 1).wait_send()
        wz_copy(i + 1).wait_send()

    loop(N - 1, ring_sent)
    wc_copy.wait_send()
    wx_copy.wait_send()


def dense(psend, pkeep, dst, cot, w_self, w_neigh):
    block, width = pkeep.shape[1:]
    hid = w_self.shape[1]
    tall = 2 * width // (4 * N)
    dma = pltpu.SemaphoreType.DMA
    return pl.pallas_call(
        dense_kernel,
        out_shape=(
            jax.ShapeDtypeStruct((block, hid), BF16),
            jax.ShapeDtypeStruct((4 * N, block, width), BF16),
            jax.ShapeDtypeStruct((tall, hid), F32),
        ),
        in_specs=[VMEM] * 6,
        out_specs=(VMEM,) * 3,
        scratch_shapes=[
            pltpu.VMEM((2 * N, block, width), BF16),
            pltpu.VMEM((N, block, width), BF16),
            pltpu.VMEM((N, block, width), BF16),
            pltpu.VMEM((N, block, width), BF16),
            pltpu.VMEM((N, block, width), BF16),
            pltpu.VMEM((block, width), F32),
            pltpu.VMEM((4 * N, tall, hid), F32),
            pltpu.VMEM((2 * N, tall, hid), F32),
            pltpu.VMEM((N, tall, hid), F32),
            pltpu.VMEM((N, tall, hid), F32),
            pltpu.VMEM((N, tall, hid), F32),
            pltpu.VMEM((N, tall, hid), F32),
            dma((2 * N,)), dma((2 * N,)), dma((N,)), dma((N,)), dma((N,)), dma((N,)),
            dma((N,)), dma((N,)), dma((N,)), dma((N,)), dma((2 * N,)), dma((2 * N,)),
            dma, dma, dma, dma, dma((N,)), dma((N,)),
        ],
        compiler_params=pltpu.CompilerParams(
            collective_id=0, has_side_effects=True, vmem_limit_bytes=LIMIT
        ),
    )(psend, pkeep, dst, cot, w_self, w_neigh)


def source_kernel(
    scale, qsend, qkeep, wpart,
    out, w_out,
    got_h, y_send, got_y, w_h, w_ys, w_y,
    h_s, h_r, y_s, y_r, wh_s, wh_r, wy_s, wy_r,
    gz_s, gz_r, gx_s, gx_r, gc_s, gc_r,
):
    row, col = lax.axis_index("row"), lax.axis_index("col")
    z, x, k = col_parts()
    y, h = row_parts()
    across = (y * 2 + (1 - h), col)
    sibling = (row, z * 4 + x * 2 + (1 - k))
    beside = (row, z * 4 + (1 - x) * 2 + k)

    def yring(d):
        other = (y + d) % N
        return other, (other * 2 + h, col)

    def zring(d):
        other = (z + d) % N
        return (row, other * 4 + x * 2 + k)

    barrier = pltpu.get_barrier_semaphore()
    for device in (across, sibling, beside):
        pl.semaphore_signal(barrier, inc=1, device_id=device, device_id_type=MESH)
    for d in range(1, N):
        pl.semaphore_signal(barrier, inc=1, device_id=yring(d)[1], device_id_type=MESH)
        pl.semaphore_signal(barrier, inc=1, device_id=zring(d), device_id_type=MESH)
    pl.semaphore_wait(barrier, 2 * N + 1)

    def h_copy(at):
        return remote(qsend.at[at], got_h.at[at], h_s.at[at], h_r.at[at], across)

    wh_copy = remote(wpart, w_h, wh_s, wh_r, across)
    wh_copy.start()
    loop(N - 1, lambda i: h_copy((y + far(i)) % N).start())
    h_copy(y).start()

    wh_copy.wait_recv()
    w_ys[...] = wpart[...] + w_h[...]
    w_y[y] = w_ys[...]

    def wy_copy(d):
        return remote(w_ys, w_y.at[y], wy_s.at[d], wy_r.at[d], yring(d)[1])

    loop(N - 1, lambda i: wy_copy(far(i)).start())

    def y_copy(d):
        other, device = yring(d)
        return remote(y_send.at[other], got_y.at[y], y_s.at[d], y_r.at[d], device)

    def y_step(i):
        d = far(i)
        other = (y + d) % N
        h_copy(other).wait_recv()
        y_send[other] = (qkeep[other] + got_h[other].astype(F32)).astype(BF16)
        y_copy(d).start()

    loop(N - 1, y_step)
    h_copy(y).wait_recv()
    out[...] = qkeep[y] + got_h[y].astype(F32)

    loop(N - 1, lambda i: wy_copy(near(i)).wait_recv())
    total = w_y[0]
    for i in range(1, N):
        total += w_y[i]
    me = k * 16 + x * N + z
    w_out[me] = total * scale

    mine = k * 16 + x * N

    def gz_copy(d):
        return remote(w_out.at[me], w_out.at[me], gz_s.at[d], gz_r.at[d], zring(d))

    def gx_copy(at):
        return remote(w_out.at[mine + at], w_out.at[mine + at], gx_s.at[at], gx_r.at[at], beside)

    def gc_copy(part, at):
        slot = k * 16 + part * N + at
        sem = part * N + at
        return remote(w_out.at[slot], w_out.at[slot], gc_s.at[sem], gc_r.at[sem], sibling)

    loop(N - 1, lambda i: gz_copy(far(i)).start())
    gx_copy(z).start()
    gc_copy(x, z).start()

    def y_take(i):
        d = near(i)
        y_copy(d).wait_recv()
        out[...] += got_y[(y + N - d) % N].astype(F32)

    def forward(i):
        d = near(i)
        other = (z + N - d) % N
        gz_copy(d).wait_recv()
        gx_copy(other).start()
        gc_copy(x, other).start()

    def gx_take(at):
        gx_copy(at).wait_recv()
        gc_copy(1 - x, at).start()

    loop(N - 1, forward)
    gx_take(z)
    loop(N - 1, lambda i: gx_take((z + near(i)) % N))
    loop(N - 1, y_take)
    loop(2 * N, lambda i: gc_copy(i // N, i % N).wait_recv())

    loop(N, lambda i: h_copy(i).wait_send())
    loop(N, lambda i: gx_copy(i).wait_send())
    loop(2 * N, lambda i: gc_copy(i // N, i % N).wait_send())

    def ring_sent(i):
        y_copy(i + 1).wait_send()
        gz_copy(i + 1).wait_send()
        wy_copy(i + 1).wait_send()

    loop(N - 1, ring_sent)
    wh_copy.wait_send()


def source(scale, qsend, qkeep, wpart):
    block, width = qkeep.shape[1:]
    tall, hid = wpart.shape
    dma = pltpu.SemaphoreType.DMA
    return pl.pallas_call(
        functools.partial(source_kernel, scale),
        out_shape=(
            jax.ShapeDtypeStruct((block, width), F32),
            jax.ShapeDtypeStruct((4 * N, tall, hid), F32),
        ),
        in_specs=[VMEM] * 3,
        out_specs=(VMEM,) * 2,
        scratch_shapes=[
            pltpu.VMEM((N, block, width), BF16),
            pltpu.VMEM((N, block, width), BF16),
            pltpu.VMEM((N, block, width), BF16),
            pltpu.VMEM((tall, hid), F32),
            pltpu.VMEM((tall, hid), F32),
            pltpu.VMEM((N, tall, hid), F32),
            dma((N,)), dma((N,)), dma((N,)), dma((N,)), dma, dma, dma((N,)), dma((N,)),
            dma((N,)), dma((N,)), dma((N,)), dma((N,)), dma((2 * N,)), dma((2 * N,)),
        ],
        compiler_params=pltpu.CompilerParams(
            collective_id=1, has_side_effects=True, vmem_limit_bytes=LIMIT
        ),
    )(qsend, qkeep, wpart)


def per_device(features, dst_features, w_self, w_neigh, cotangent, block_values, block_rows, block_cols, block_counts):
    block = block_values.shape[-1]
    width = features.shape[-1]
    vals = block_values[0, 0]
    table = features.reshape(-1, block, width)
    psend, pkeep = products(forward_kernel, 2 * N, block_rows, block_cols, block_counts, table, vals)
    out, grads, wpart = dense(psend, pkeep, dst_features, cotangent, w_self, w_neigh)
    qsend, qkeep = products(backward_kernel, N, block_rows, block_cols, block_counts, grads, vals)
    nodes = dst_features.shape[0] * lax.axis_size("row") * lax.axis_size("col")
    source_part, w_all = source(1.0 / math.sqrt(nodes), qsend, qkeep, wpart)
    w_all = w_all.reshape(2, width, -1)
    return out, w_all[0], w_all[1], source_part[None]


def solution(mesh):
    placed = (
        P("col", None, None),
        P(("row", "col"), None),
        P(),
        P(),
        P(("row", "col"), None),
        P("row", "col", None, None, None),
        P("row", "col", None),
        P("row", "col", None),
        P("row", "col"),
    )
    return jax.shard_map(
        per_device,
        mesh=mesh,
        in_specs=placed,
        out_specs=(P(("row", "col"), None), P(), P(), P("col", "row", None)),
        check_vma=False,
    )
```

time: 702 us -> 79.3 us (0.11)
  waiting for transfers between devices: 655 us -> 0 us
  Pallas kernels: 0 us -> 72.8 us
  between operations: 14.6 us -> 1.38 us
  matrix products: 11.2 us -> 0 us
  local copies, waits for them, and re-layouts: 14.7 us -> 4.92 us
    reduce_scatter x2 -> x0, waiting for transfers between devices: 325 us -> none  [the longest x1 201 us: per_device(): lax.psum_scatter(source_terms, 'row', scatter_dimension=0, tiled=True)]
    psum x1 -> x0, waiting for transfers between devices: 265 us -> none  [per_device(): self_sum, neigh_sum = lax.psum((self_grad, neigh_grad), ('row', 'col'))]
    pallas_call x0 -> x4, Pallas kernels: none -> 72.8 us  [the longest x1 44.9 us: dense(): pl.pallas_call(dense_kernel, out_shape=(jax.ShapeDtypeStruct((block, hid)...]
    all_gather x1 -> x0, waiting for transfers between devices: 65.6 us -> none  [per_device(): slab_grad = lax.all_gather(local_grad, 'col', axis=0, tiled=True)]
    dot_general x9 -> x0, matrix products: 11.2 us -> none  [the longest x2 4.09 us: slot_products(): jnp.einsum(einsum_form, block_vals, source_table[slot_index], preferred_e...]
    dot_general x4 -> x0, local copies, waits for them, and re-layouts: 8.63 us -> none  [the longest x2 4.77 us: slot_products(): jnp.einsum(einsum_form, block_vals, source_table[slot_index], preferred_e...]
  transfers between devices with their start and end apart: 4 -> 0, of which waited for: 4 -> 0; matrix products, arithmetic and copies ran while one was open for 2% -> 0% of each run, Pallas kernels for 0% -> 0%
where the time goes in v1:
time: 79.3 us; the launch traced here: 79.1 us
  Pallas kernels  72.8 us (92%)
  local copies, waits for them, and re-layouts  4.92 us (6%)
  between operations  1.38 us (2%)
    pallas_call x1, Pallas kernels, dense(): pl.pallas_call(dense_kernel, out_shape=(jax.ShapeDtypeStruct((block, hid)...  44.9 us
    pallas_call x1, Pallas kernels, source(): pl.pallas_call(functools.partial(source_kernel, scale), out_shape=(jax.Sh...  25 us
    unnamed x20, local copies, waits for them, and re-layouts  4.2 us
    pallas_call x2, Pallas kernels, products(): pl.pallas_call(kernel, out_shape=(jax.ShapeDtypeStruct((half, block, widt...  2.91 us

profile of v1, /device:TPU:1, one launch (start us, length us, event | category | flops | bytes accessed | tf_op | source)
XLA Modules:
  0.0 79.1 jit_solution(12910822071145982135)
XLA Ops:
  1.3 0.0 copy-start.7
  1.3 0.0 copy-start.8
  1.3 0.6 copy-done.7
  1.9 0.0 copy-done.8
  2.0 0.0 copy-start
  2.0 1.2 %copy-done = bf16[1,1,32,128,128]{4,3,2,1,0:T(8,128)(2,1)S(1)} copy-done((bf16[1,1,32,128,128]{4,3,2,1,0:T(8,128)(2,1)S(1)}, bf16[1,1,32,128,128]{4,3,2,1,0:T(8,128)(2,1)}, u32[]{:S(2)}) %copy-start) | copy-done | bytes 1048600
  3.2 0.0 copy-start.2
  3.2 1.0 %copy-done.2 = bf16[1,2048,128]{2,1,0:T(8,128)(2,1)S(1)} copy-done((bf16[1,2048,128]{2,1,0:T(8,128)(2,1)S(1)}, bf16[1,2048,128]{2,1,0:T(8,128)(2,1)}, u32[]{:S(2)}) %copy-start.2) | copy-done | bytes 524312
  4.2 0.0 copy-start.3
  4.2 0.0 copy-start.4
  4.2 0.0 copy-start.5
  4.2 0.0 copy-start.6
  4.2 1.5 %shard_map.120 = (bf16[16,128,128]{2,1,0:T(8,128)(2,1)S(1)}, f32[16,128,128]{2,1,0:T(8,128)S(1)}) custom-call(s32[1,1,32]{2,1,0:T(1,128)S(1)} %copy-done.7, s32[1,1,32]{2,1,0:T(1,128)S(1)} %copy-done.8, s32[1,1]{1,0:T(1,128)S(6)} %copy.15.counts, bf16[16,128,128]{2,1,0:T(8,128)(2,1)S(1)} %bitcast.9, bf16[32,128,128]{2,1,0:T(8,128)(2,1)S(1)} %bitcast.7), custom_call_target="tpu_custom_call" | custom-call | flops 134217728 | bytes 2621440 | tf_op jit(solution)/shard_map/pallas_call | solution.py:84
  5.7 0.0 copy-start.1
  5.7 0.0 copy-done.3
  5.7 0.0 copy-done.4
  5.7 0.0 copy-done.5
  5.8 0.0 copy-done.6
  5.8 44.9 %shard_map.121 = (bf16[128,256]{1,0:T(8,128)(2,1)S(1)}, bf16[32,128,128]{2,1,0:T(8,128)(2,1)S(1)}, f32[8,256]{1,0:T(8,128)S(1)}) custom-call(bf16[16,128,128]{2,1,0:T(8,128)(2,1)S(1)} %get-tuple-element.13.psend, f32[16,128,128]{2,1,0:T(8,128)S(1)} %get-tuple-element.14.pkeep, bf16[128,128]{1,0:T(8,128)(2,1)S(1)} %copy-done.6, ...), custom_call_target="tpu_custom_call" | custom-call | tf_op jit(solution)/shard_map/pallas_call | solution.py:282
  50.6 0.0 copy-done.1
  50.6 1.4 %shard_map.122 = (bf16[8,128,128]{2,1,0:T(8,128)(2,1)S(1)}, f32[8,128,128]{2,1,0:T(8,128)S(1)}) custom-call(s32[1,1,32]{2,1,0:T(1,128)S(1)} %copy-done.7, s32[1,1,32]{2,1,0:T(1,128)S(1)} %copy-done.8, s32[1,1]{1,0:T(1,128)S(6)} %copy.15.counts, bf16[32,128,128]{2,1,0:T(8,128)(2,1)S(1)} %get-tuple-element.16.grads, bf16[32,128,128]{2,1,0:T(8,128)(2,1)S(1)} %bitcast.8), custom_call_target="tpu_custom_call" | custom-call | flops 134217728 | bytes 1835008 | tf_op jit(solution)/shard_map/pallas_call | solution.py:84
  52.1 25.0 %shard_map.123 = (f32[128,128]{1,0:T(8,128)S(1)}, f32[32,8,256]{2,1,0:T(8,128)S(1)}) custom-call(bf16[8,128,128]{2,1,0:T(8,128)(2,1)S(1)} %get-tuple-element.17.qsend, f32[8,128,128]{2,1,0:T(8,128)S(1)} %get-tuple-element.18.qkeep, f32[8,256]{1,0:T(8,128)S(1)} %get-tuple-element.19.wpart), custom_call_target="tpu_custom_call" | custom-call | tf_op jit(solution)/shard_map/pallas_call | solution.py:439
  77.1 0.7 slice_bitcast_fusion
  77.8 0.6 copy.16
  78.5 0.6 copy.17
Async XLA Ops:
  1.3 0.7 copy-start.7
  1.3 0.7 copy-start.8
  2.0 1.2 %copy-start = (bf16[1,1,32,128,128]{4,3,2,1,0:T(8,128)(2,1)S(1)}, bf16[1,1,32,128,128]{4,3,2,1,0:T(8,128)(2,1)}, u32[]{:S(2)}) copy-start(bf16[1,1,32,128,128]{4,3,2,1,0:T(8,128)(2,1)} %param.14) | copy-start | bytes 3145732
  3.2 1.0 %copy-start.2 = (bf16[1,2048,128]{2,1,0:T(8,128)(2,1)S(1)}, bf16[1,2048,128]{2,1,0:T(8,128)(2,1)}, u32[]{:S(2)}) copy-start(bf16[1,2048,128]{2,1,0:T(8,128)(2,1)} %param.9) | copy-start | bytes 1572868
  4.2 1.5 %copy-start.3 = (bf16[128,256]{1,0:T(8,128)(2,1)S(1)}, bf16[128,256]{1,0:T(8,128)(2,1)}, u32[]{:S(2)}) copy-start(bf16[128,256]{1,0:T(8,128)(2,1)} %cot.1) | copy-start | bytes 196612
  4.2 1.5 %copy-start.4 = (bf16[128,256]{1,0:T(8,128)(2,1)S(1)}, bf16[128,256]{1,0:T(8,128)(2,1)}, u32[]{:S(2)}) copy-start(bf16[128,256]{1,0:T(8,128)(2,1)} %w_self.1) | copy-start | bytes 196612
  4.2 1.5 %copy-start.5 = (bf16[128,256]{1,0:T(8,128)(2,1)S(1)}, bf16[128,256]{1,0:T(8,128)(2,1)}, u32[]{:S(2)}) copy-start(bf16[128,256]{1,0:T(8,128)(2,1)} %w_neigh.1) | copy-start | bytes 196612
  4.2 1.5 %copy-start.6 = (bf16[128,128]{1,0:T(8,128)(2,1)S(1)}, bf16[128,128]{1,0:T(8,128)(2,1)}, u32[]{:S(2)}) copy-start(bf16[128,128]{1,0:T(8,128)(2,1)} %dst.1) | copy-start | bytes 98308
  5.7 44.9 %copy-start.1 = (bf16[1,1,32,128,128]{4,3,2,1,0:T(8,128)(2,1)S(1)}, bf16[1,1,32,128,128]{4,3,2,1,0:T(8,128)(2,1)}, u32[]{:S(2)}) copy-start(bf16[1,1,32,128,128]{4,3,2,1,0:T(8,128)(2,1)} %param.14) | copy-start | bytes 3145732

commit v2 on v0

v2 whole, which is shorter than its diff:
```python
import functools
import math

import jax
import jax.numpy as jnp
from jax import lax
from jax.experimental import pallas as pl
from jax.experimental.pallas import tpu as pltpu
from jax.sharding import PartitionSpec as P

BF16 = jnp.bfloat16
F32 = jnp.float32
MESH = pl.DeviceIdType.MESH
N = 8
OFFSETS = (4, 3, 5, 2, 6, 1, 7, 0)
VMEM = pl.BlockSpec(memory_space=pltpu.VMEM)
SMEM = pl.BlockSpec(memory_space=pltpu.SMEM)
HBM = pl.BlockSpec(memory_space=pltpu.HBM)
DMA = pltpu.SemaphoreType.DMA


def remote(src, dst, send, recv, device):
    return pltpu.make_async_remote_copy(
        src_ref=src, dst_ref=dst, send_sem=send, recv_sem=recv, device_id=device, device_id_type=MESH
    )


def chain_kernel(rows, cols, counts, row_prev, row_last, col_prev, col_last):
    slots = row_prev.shape[0]
    live = counts[0, 0]
    for last in (row_last, col_last):
        for b in range(last.shape[0]):
            last[b] = slots
    for s in range(slots):
        for ids, prev, last in ((rows, row_prev, row_last), (cols, col_prev, col_last)):
            b = ids[0, 0, s]
            before = last[b]
            prev[s] = before
            last[b] = jnp.where(s < live, s, before)


def chains(rows, cols, counts, row_blocks, col_blocks):
    slots = rows.shape[-1]
    return pl.pallas_call(
        chain_kernel,
        out_shape=tuple(jax.ShapeDtypeStruct((n,), jnp.int32) for n in (slots, row_blocks, slots, col_blocks)),
        in_specs=[SMEM] * 3,
        out_specs=(SMEM,) * 4,
    )(rows, cols, counts)


def ring_reduce(piece, ahead, behind, sent, got_a, got_b, a_s, a_r, b_s, b_r):
    tall = sent.shape[1] // 2
    top, low = pl.ds(0, tall), pl.ds(tall, tall)

    def a_copy(hop):
        if hop == 0:
            return remote(sent.at[0, top], got_a.at[0, top], a_s.at[0], a_r.at[0], ahead)
        return remote(sent.at[2 * hop - 1], got_a.at[hop], a_s.at[hop], a_r.at[hop], ahead)

    def b_copy(hop):
        if hop == 0:
            return remote(sent.at[0, low], got_b.at[0, low], b_s.at[0], b_r.at[0], behind)
        return remote(sent.at[2 * hop], got_b.at[hop], b_s.at[hop], b_r.at[hop], behind)

    sent[0] = piece(0).astype(BF16)
    a_copy(0).start()
    b_copy(0).start()
    part = piece(1)
    sent[1, low] = part[tall:].astype(BF16)
    a_copy(0).wait_recv()
    sent[1, top] = (part[:tall] + got_a[0, top].astype(F32)).astype(BF16)
    a_copy(1).start()
    part = piece(2)
    sent[2, top] = part[:tall].astype(BF16)
    b_copy(0).wait_recv()
    sent[2, low] = (part[tall:] + got_b[0, low].astype(F32)).astype(BF16)
    b_copy(1).start()
    yield
    for hop in (2, 3):
        part = piece(2 * hop - 1)
        a_copy(hop - 1).wait_recv()
        sent[2 * hop - 1] = (part + got_a[hop - 1].astype(F32)).astype(BF16)
        a_copy(hop).start()
        part = piece(2 * hop)
        b_copy(hop - 1).wait_recv()
        sent[2 * hop] = (part + got_b[hop - 1].astype(F32)).astype(BF16)
        b_copy(hop).start()
        yield
    part = piece(7)
    a_copy(3).wait_recv()
    b_copy(3).wait_recv()
    total = part + got_a[3].astype(F32) + got_b[3].astype(F32)
    yield total
    for hop in range(4):
        a_copy(hop).wait_send()
        b_copy(hop).wait_send()
    yield


def layer_kernel(
    scale,
    row_prev, row_last, col_prev, col_last, rows, cols,
    feats_h, vals_h, dst_h, cot_h, w_self_h, w_neigh_h,
    out, w_out, source,
    feats, vals, dst, cot, w_self, w_neigh, sums, grads,
    c_send, got_c, x_send, got_x, z_sent, z_a, z_b,
    h_send, got_h, y_sent, y_a, y_b,
    w_full, w_c, w_xs, w_x, w_zs, w_z, w_mine, w_rows,
    load_sem,
    c_s, c_r, x_s, x_r, za_s, za_r, zb_s, zb_r, h_s, h_r, ya_s, ya_r, yb_s, yb_r,
    ga_s, ga_r, gb_s, gb_r, gx_s, gx_r, gc_s, gc_r,
    wc_s, wc_r, wx_s, wx_r, wz_s, wz_r, wr_s, wr_r, wg_s, wg_r, wl_s, wl_r,
):
    row, col = lax.axis_index("row"), lax.axis_index("col")
    z, x, k = col // 4, (col // 2) % 2, col % 2
    y, h = row // 2, row % 2
    slots = vals.shape[0]
    quarter = slots // 4

    def at_col(zz, xx, kk):
        return (row, (zz % N) * 4 + xx * 2 + kk)

    def at_row(yy, hh):
        return ((yy % N) * 2 + hh, col)

    sibling, beside, across = at_col(z, x, 1 - k), at_col(z, 1 - x, k), at_row(y, 1 - h)

    def near(i):
        return at_col(z + i % N, (x + i // N) % 2, k)

    def far(i):
        return at_row(y + i % N, (h + i // N) % 2)

    barrier = pltpu.get_barrier_semaphore()

    def greet(i, c):
        pl.semaphore_signal(barrier, inc=1, device_id=near(i), device_id_type=MESH)
        pl.semaphore_signal(barrier, inc=1, device_id=far(i), device_id_type=MESH)
        return c

    pl.semaphore_signal(barrier, inc=1, device_id=sibling, device_id_type=MESH)
    lax.fori_loop(1, 2 * N, greet, 0)

    loads = [pltpu.make_async_copy(feats_h, feats, load_sem.at[0])]
    for i in range(4):
        part = pl.ds(i * quarter, quarter)
        loads.append(pltpu.make_async_copy(vals_h.at[part], vals.at[part], load_sem.at[1 + i]))
    for i, (src, dest) in enumerate(((dst_h, dst), (w_self_h, w_self), (w_neigh_h, w_neigh), (cot_h, cot))):
        loads.append(pltpu.make_async_copy(src, dest, load_sem.at[5 + i]))
    for load in loads:
        load.start()

    sums[slots] = jnp.zeros_like(sums[slots])
    loads[0].wait()
    for s in range(slots):
        if s % quarter == 0:
            loads[1 + s // quarter].wait()
        sums[s] = sums[row_prev[s]] + jnp.dot(vals[s], feats[cols[0, 0, s]], preferred_element_type=F32)

    def partial(zz, xx, kk):
        return sums[row_last[(zz % N) * 4 + xx * 2 + kk]]

    pl.semaphore_wait(barrier, 4 * N - 1)

    def c_copy(i):
        return remote(c_send.at[i], got_c.at[i], c_s.at[i], c_r.at[i], sibling)

    for i in range(2 * N):
        c_send[i] = partial(z + OFFSETS[i % N], 1 - x if i < N else x, 1 - k).astype(BF16)
        c_copy(i).start()

    def x_copy(i):
        return remote(x_send.at[i], got_x.at[i], x_s.at[i], x_r.at[i], beside)

    for i in range(N):
        own = partial(z + OFFSETS[i], 1 - x, k)
        c_copy(i).wait_recv()
        x_send[i] = (own + got_c[i].astype(F32)).astype(BF16)
        x_copy(i).start()

    for load in loads[5:]:
        load.wait()
    pre_self = jnp.dot(dst[...], w_self[...], preferred_element_type=F32)

    def col_piece(i):
        own = partial(z + OFFSETS[i], x, k)
        c_copy(N + i).wait_recv()
        own += got_c[N + i].astype(F32)
        x_copy(i).wait_recv()
        return own + got_x[i].astype(F32)

    z_next, z_back = at_col(z + 1, x, k), at_col(z + N - 1, x, k)
    z_ring = ring_reduce(col_piece, z_next, z_back, z_sent, z_a, z_b, za_s, za_r, zb_s, zb_r)
    for _ in range(3):
        next(z_ring)
    agg = next(z_ring).astype(BF16)

    pre = pre_self + jnp.dot(agg, w_neigh[...], preferred_element_type=F32)
    sig = jax.nn.sigmoid(pre)
    gpre = (cot[...].astype(F32) * sig * (1.0 + pre * (1.0 - sig))).astype(BF16)
    mine = k * 2 * N + x * N
    me = mine + z
    grads[me] = lax.dot_general(
        gpre, w_neigh[...], (((1,), (1,)), ((), ())), preferred_element_type=F32
    ).astype(BF16)

    tall = grads.shape[1] // 2
    top, low = pl.ds(0, tall), pl.ds(tall, tall)

    def ga_copy(hop):
        slot = mine + (z + N - hop) % N
        ref = grads.at[slot, top] if hop == 3 else grads.at[slot]
        return remote(ref, ref, ga_s.at[hop], ga_r.at[hop], z_next)

    def gb_copy(hop):
        slot = mine + (z + hop) % N
        ref = grads.at[slot, low] if hop == 3 else grads.at[slot]
        return remote(ref, ref, gb_s.at[hop], gb_r.at[hop], z_back)

    def gx_copy(off):
        ref = grads.at[mine + (z + off) % N]
        return remote(ref, ref, gx_s.at[off], gx_r.at[off], beside)

    def gc_copy(other, off):
        ref = grads.at[k * 2 * N + ((x + other) % 2) * N + (z + off) % N]
        return remote(ref, ref, gc_s.at[other * N + off], gc_r.at[other * N + off], sibling)

    def spread(off):
        gx_copy(off).start()
        gc_copy(0, off).start()

    def from_beside(off):
        gx_copy(off).wait_recv()
        gc_copy(1, off).start()

    ga_copy(0).start()
    gb_copy(0).start()
    spread(0)
    out[...] = (pre * sig).astype(BF16)

    feat = dst.shape[1]
    pieces, wide, hid = w_full.shape
    half = pieces // 2
    for base, left in ((0, dst[...]), (1, agg)):
        dw = lax.dot_general(left, gpre, (((0,), (0,)), ((), ())), preferred_element_type=F32)
        w_full[pl.ds(base * half, half)] = dw.reshape(half, wide, hid)
    wc_copy = remote(w_full.at[pl.ds((1 - k) * half, half)], w_c, wc_s, wc_r, sibling)
    wc_copy.start()

    for hop in (1, 2, 3):
        ga_copy(hop - 1).wait_recv()
        ga_copy(hop).start()
        spread(N - hop)
        gb_copy(hop - 1).wait_recv()
        gb_copy(hop).start()
        spread(hop)
        if hop == 1:
            from_beside(0)
            wc_copy.wait_recv()
            w_xs[...] = w_full[pl.ds(k * half + (1 - x) * N, N)] + w_c[pl.ds((1 - x) * N, N)]
            wx_copy = remote(w_xs, w_x, wx_s, wx_r, beside)
            wx_copy.start()
        else:
            from_beside(N - hop + 1)
            from_beside(hop - 1)
    wx_copy.wait_recv()
    w_zs[...] = w_full[pl.ds(k * half + x * N, N)] + w_c[pl.ds(x * N, N)] + w_x[...]

    def wz_copy(d):
        ref = w_zs.at[(z + d) % N]
        return remote(ref, w_z.at[z], wz_s.at[d], wz_r.at[d], near(d))

    for d in OFFSETS[:-1]:
        wz_copy(d).start()
    ga_copy(3).wait_recv()
    gb_copy(3).wait_recv()
    spread(4)
    for off in (5, 3, 4):
        from_beside(off)
    for i in range(2 * N):
        gc_copy(i // N, i % N).wait_recv()

    for s in range(slots):
        r = rows[0, 0, s]
        g = grads[(r % 2) * 2 * N + ((r // 2) % 2) * N + r // 4]
        sums[s] = sums[col_prev[s]] + lax.dot_general(
            vals[s], g, (((0,), (0,)), ((), ())), preferred_element_type=F32
        )

    def source_partial(yy, hh):
        return sums[col_last[(yy % N) * 2 + hh]]

    def h_copy(i):
        return remote(h_send.at[i], got_h.at[i], h_s.at[i], h_r.at[i], across)

    for i in range(N):
        h_send[i] = source_partial(y + OFFSETS[i], 1 - h).astype(BF16)
        h_copy(i).start()

    total = w_zs[z]
    for d in range(1, N):
        wz_copy(d).wait_recv()
        total += w_z[(z + N - d) % N]
    w_mine[...] = total
    w_rows[row] = total

    def wr_copy(i):
        return remote(w_mine, w_rows.at[row], wr_s.at[i], wr_r.at[i], far(i))

    for i in range(1, 2 * N):
        wr_copy(i).start()

    def row_piece(i):
        own = source_partial(y + OFFSETS[i], h)
        h_copy(i).wait_recv()
        return own + got_h[i].astype(F32)

    y_ring = ring_reduce(
        row_piece, at_row(y + 1, h), at_row(y + N - 1, h), y_sent, y_a, y_b, ya_s, ya_r, yb_s, yb_r
    )
    for _ in range(3):
        next(y_ring)
    for i in range(1, 2 * N):
        wr_copy(i).wait_recv()
    total = w_rows[0]
    for i in range(1, 2 * N):
        total += w_rows[i]
    w_out[me] = total * scale

    def wg_copy(i):
        return remote(w_out.at[me], w_out.at[me], wg_s.at[i], wg_r.at[i], near(i))

    for i in range(1, 2 * N):
        wg_copy(i).start()
    source[...] = next(y_ring)
    for i in range(1, 2 * N):
        wg_copy(i).wait_recv()
    ref = w_out.at[pl.ds(k * half, half)]
    wl_copy = remote(ref, ref, wl_s, wl_r, sibling)
    wl_copy.start()

    next(z_ring)
    next(y_ring)
    for i in range(N):
        x_copy(i).wait_send()
        h_copy(i).wait_send()
        gx_copy(i).wait_send()
    for hop in range(4):
        ga_copy(hop).wait_send()
        gb_copy(hop).wait_send()
    for i in range(2 * N):
        c_copy(i).wait_send()
        gc_copy(i // N, i % N).wait_send()
    wc_copy.wait_send()
    wx_copy.wait_send()
    for d in range(1, N):
        wz_copy(d).wait_send()
    for i in range(1, 2 * N):
        wr_copy(i).wait_send()
        wg_copy(i).wait_send()
    wl_copy.wait()


def layer(scale, tables, rows, cols, feats, vals, dst, cot, w_self, w_neigh):
    slots, block, _ = vals.shape
    width = feats.shape[-1]
    hid = w_self.shape[1]
    wide = 2 * width // (4 * N)

    def blocks(n, kind=BF16):
        return pltpu.VMEM((n, block, width), kind)

    def slabs(n):
        return pltpu.VMEM((n, wide, hid), F32)

    return pl.pallas_call(
        functools.partial(layer_kernel, scale),
        out_shape=(
            jax.ShapeDtypeStruct((block, hid), BF16),
            jax.ShapeDtypeStruct((4 * N, wide, hid), F32),
            jax.ShapeDtypeStruct((block, width), F32),
        ),
        in_specs=[SMEM] * 6 + [HBM] * 6,
        out_specs=(VMEM,) * 3,
        scratch_shapes=[
            blocks(feats.shape[0]), pltpu.VMEM(vals.shape, BF16), pltpu.VMEM(dst.shape, BF16),
            pltpu.VMEM(cot.shape, BF16), pltpu.VMEM(w_self.shape, BF16), pltpu.VMEM(w_neigh.shape, BF16),
            blocks(slots + 1, F32), blocks(4 * N),
            blocks(2 * N), blocks(2 * N), blocks(N), blocks(N), blocks(N - 1), blocks(4), blocks(4),
            blocks(N), blocks(N), blocks(N - 1), blocks(4), blocks(4),
            slabs(4 * N), slabs(2 * N), slabs(N), slabs(N), slabs(N), slabs(N),
            pltpu.VMEM((wide, hid), F32), slabs(2 * N),
            DMA((9,)),
            DMA((2 * N,)), DMA((2 * N,)), DMA((N,)), DMA((N,)), DMA((4,)), DMA((4,)), DMA((4,)), DMA((4,)),
            DMA((N,)), DMA((N,)), DMA((4,)), DMA((4,)), DMA((4,)), DMA((4,)),
            DMA((4,)), DMA((4,)), DMA((4,)), DMA((4,)), DMA((N,)), DMA((N,)), DMA((2 * N,)), DMA((2 * N,)),
            DMA, DMA, DMA, DMA, DMA((N,)), DMA((N,)), DMA((2 * N,)), DMA((2 * N,)), DMA((2 * N,)), DMA((2 * N,)),
            DMA, DMA,
        ],
        compiler_params=pltpu.CompilerParams(
            collective_id=0, has_side_effects=True, vmem_limit_bytes=40 * 1024 * 1024
        ),
    )(*tables, rows, cols, feats, vals, dst, cot, w_self, w_neigh)


def per_device(features, dst_features, w_self, w_neigh, cotangent, block_values, block_rows, block_cols, block_counts):
    block = block_values.shape[-1]
    width = features.shape[-1]
    tables = chains(block_rows, block_cols, block_counts, 4 * N, 2 * N)
    nodes = dst_features.shape[0] * lax.axis_size("row") * lax.axis_size("col")
    out, w_all, source = layer(
        1.0 / math.sqrt(nodes), tables, block_rows, block_cols, features.reshape(-1, block, width),
        block_values[0, 0], dst_features, cotangent, w_self, w_neigh,
    )
    w_all = w_all.reshape(2, width, -1)
    return out, w_all[0], w_all[1], source[None]


def solution(mesh):
    placed = (
        P("col", None, None),
        P(("row", "col"), None),
        P(),
        P(),
        P(("row", "col"), None),
        P("row", "col", None, None, None),
        P("row", "col", None),
        P("row", "col", None),
        P("row", "col"),
    )
    return jax.shard_map(
        per_device,
        mesh=mesh,
        in_specs=placed,
        out_specs=(P(("row", "col"), None), P(), P(), P("col", "row", None)),
        check_vma=False,
    )
```

time: 702 us -> 83.7 us (0.12)
  waiting for transfers between devices: 655 us -> 0 us
  Pallas kernels: 0 us -> 73.7 us
  between operations: 14.6 us -> 1.35 us
  matrix products: 11.2 us -> 0 us
    reduce_scatter x2 -> x0, waiting for transfers between devices: 325 us -> none  [the longest x1 201 us: per_device(): lax.psum_scatter(source_terms, 'row', scatter_dimension=0, tiled=True)]
    psum x1 -> x0, waiting for transfers between devices: 265 us -> none  [per_device(): self_sum, neigh_sum = lax.psum((self_grad, neigh_grad), ('row', 'col'))]
    pallas_call x0 -> x2, Pallas kernels: none -> 73.7 us  [the longest x1 72.3 us: layer(): pl.pallas_call(functools.partial(layer_kernel, scale), out_shape=(jax.Sha...]
    all_gather x1 -> x0, waiting for transfers between devices: 65.6 us -> none  [per_device(): slab_grad = lax.all_gather(local_grad, 'col', axis=0, tiled=True)]
    dot_general x9 -> x0, matrix products: 11.2 us -> none  [the longest x2 4.09 us: slot_products(): jnp.einsum(einsum_form, block_vals, source_table[slot_index], preferred_e...]
    dot_general x4 -> x0, local copies, waits for them, and re-layouts: 8.63 us -> none  [the longest x2 4.77 us: slot_products(): jnp.einsum(einsum_form, block_vals, source_table[slot_index], preferred_e...]
  transfers between devices with their start and end apart: 4 -> 0, of which waited for: 4 -> 0; matrix products, arithmetic and copies ran while one was open for 2% -> 0% of each run, Pallas kernels for 0% -> 0%
where the time goes in v2:
time: 83.7 us; the launch traced here: 83.3 us
  Pallas kernels  73.7 us (88%)
  local copies, waits for them, and re-layouts  8.2 us (10%)
  between operations  1.35 us (2%)
    pallas_call x1, Pallas kernels, layer(): pl.pallas_call(functools.partial(layer_kernel, scale), out_shape=(jax.Sha...  72.3 us
    unnamed x26, local copies, waits for them, and re-layouts  7.48 us

profile of v2, /device:TPU:1, one launch (start us, length us, event | category | flops | bytes accessed | tf_op | source)
XLA Modules:
  0.0 83.3 jit_solution(908721630788986894)
XLA Ops:
  1.3 1.4 %shard_map.120 = (s32[32]{0:T(128)}, s32[32]{0:T(128)}, s32[32]{0:T(128)}, s32[16]{0:T(128)}) custom-call(s32[1,1,32]{2,1,0:T(1,128)} %rows.3, s32[1,1,32]{2,1,0:T(1,128)} %cols.3, s32[1,1]{1,0:T(1,128)S(6)} %copy.15.counts), custom_call_target="tpu_custom_call" | custom-call | tf_op jit(solution)/shard_map/pallas_call | solution.py:44
  2.7 0.0 copy-start.9
  2.7 0.0 copy-start.10
  2.7 0.0 copy-start.11
  2.7 0.0 copy-start.6
  2.7 0.0 copy-start.7
  2.8 0.0 copy-start.8
  2.8 0.6 copy-done.9
  3.4 0.0 copy-done.10
  3.4 0.0 copy-done.11
  3.4 0.0 copy-done.6
  3.4 0.0 copy-done.7
  3.4 0.0 copy-done.8
  3.4 0.0 copy-start
  3.4 1.2 %copy-done = bf16[1,1,32,128,128]{4,3,2,1,0:T(8,128)(2,1)S(1)} copy-done((bf16[1,1,32,128,128]{4,3,2,1,0:T(8,128)(2,1)S(1)}, bf16[1,1,32,128,128]{4,3,2,1,0:T(8,128)(2,1)}, u32[]{:S(2)}) %copy-start) | copy-done | bytes 1048600
  4.7 0.0 copy-start.1
  4.7 1.0 %copy-done.1 = bf16[1,2048,128]{2,1,0:T(8,128)(2,1)S(1)} copy-done((bf16[1,2048,128]{2,1,0:T(8,128)(2,1)S(1)}, bf16[1,2048,128]{2,1,0:T(8,128)(2,1)}, u32[]{:S(2)}) %copy-start.1) | copy-done | bytes 524312
  5.7 0.0 copy-start.2
  5.7 0.8 %copy-done.2 = bf16[128,256]{1,0:T(8,128)(2,1)S(1)} copy-done((bf16[128,256]{1,0:T(8,128)(2,1)S(1)}, bf16[128,256]{1,0:T(8,128)(2,1)}, u32[]{:S(2)}) %copy-start.2) | copy-done | bytes 65560
  6.5 0.0 copy-start.3
  6.5 0.8 %copy-done.3 = bf16[128,256]{1,0:T(8,128)(2,1)S(1)} copy-done((bf16[128,256]{1,0:T(8,128)(2,1)S(1)}, bf16[128,256]{1,0:T(8,128)(2,1)}, u32[]{:S(2)}) %copy-start.3) | copy-done | bytes 65560
  7.4 0.0 copy-start.4
  7.4 0.8 %copy-done.4 = bf16[128,256]{1,0:T(8,128)(2,1)S(1)} copy-done((bf16[128,256]{1,0:T(8,128)(2,1)S(1)}, bf16[128,256]{1,0:T(8,128)(2,1)}, u32[]{:S(2)}) %copy-start.4) | copy-done | bytes 65560
  8.2 0.0 copy-start.5
  8.2 0.8 copy-done.5
  9.0 72.3 %shard_map.121 = (bf16[128,256]{1,0:T(8,128)(2,1)S(1)}, f32[32,8,256]{2,1,0:T(8,128)S(1)}, f32[128,128]{1,0:T(8,128)S(1)}) custom-call(s32[32]{0:T(128)S(1)} %copy-done.8, s32[32]{0:T(128)S(1)} %copy-done.9, s32[32]{0:T(128)S(1)} %copy-done.10, s32[16]{0:T(128)S(1)} %copy-done.11, s32[1,1,32]{2,1,0:T(1,128)S(1)} %copy-done.6, s32[1,1,32]{2,1,0:T(1,128)S(1)} %copy-done.7, ...), custom_call_target="tpu_custom_call" | custom-call | tf_op jit(solution)/shard_map/pallas_call | solution.py:377
  81.3 0.7 slice_bitcast_fusion
  82.0 0.6 copy.16
  82.7 0.6 copy.17
Async XLA Ops:
  2.7 0.7 copy-start.9
  2.7 0.7 copy-start.10
  2.7 0.7 copy-start.11
  2.7 0.7 copy-start.6
  2.7 0.7 copy-start.7
  2.8 0.7 copy-start.8
  3.4 1.2 %copy-start = (bf16[1,1,32,128,128]{4,3,2,1,0:T(8,128)(2,1)S(1)}, bf16[1,1,32,128,128]{4,3,2,1,0:T(8,128)(2,1)}, u32[]{:S(2)}) copy-start(bf16[1,1,32,128,128]{4,3,2,1,0:T(8,128)(2,1)} %param.14) | copy-start | bytes 3145732
  4.7 1.0 %copy-start.1 = (bf16[1,2048,128]{2,1,0:T(8,128)(2,1)S(1)}, bf16[1,2048,128]{2,1,0:T(8,128)(2,1)}, u32[]{:S(2)}) copy-start(bf16[1,2048,128]{2,1,0:T(8,128)(2,1)} %param.9) | copy-start | bytes 1572868
  5.7 0.8 %copy-start.2 = (bf16[128,256]{1,0:T(8,128)(2,1)S(1)}, bf16[128,256]{1,0:T(8,128)(2,1)}, u32[]{:S(2)}) copy-start(bf16[128,256]{1,0:T(8,128)(2,1)} %cot_h.1) | copy-start | bytes 196612
  6.5 0.8 %copy-start.3 = (bf16[128,256]{1,0:T(8,128)(2,1)S(1)}, bf16[128,256]{1,0:T(8,128)(2,1)}, u32[]{:S(2)}) copy-start(bf16[128,256]{1,0:T(8,128)(2,1)} %w_self_h.1) | copy-start | bytes 196612
  7.4 0.8 %copy-start.4 = (bf16[128,256]{1,0:T(8,128)(2,1)S(1)}, bf16[128,256]{1,0:T(8,128)(2,1)}, u32[]{:S(2)}) copy-start(bf16[128,256]{1,0:T(8,128)(2,1)} %w_neigh_h.1) | copy-start | bytes 196612
  8.2 0.8 copy-start.5

commit v3 on v2

v3 whole, which is shorter than its diff:
```python
import functools
import math

import jax
import jax.numpy as jnp
from jax import lax
from jax.experimental import pallas as pl
from jax.experimental.pallas import tpu as pltpu
from jax.sharding import PartitionSpec as P

BF16 = jnp.bfloat16
F32 = jnp.float32
MESH = pl.DeviceIdType.MESH
N = 8
OFFSETS = (4, 3, 5, 2, 6, 1, 7, 0)
SPREAD = (1, 7, 2, 6, 3, 5, 4)
VMEM = pl.BlockSpec(memory_space=pltpu.VMEM)
SMEM = pl.BlockSpec(memory_space=pltpu.SMEM)
HBM = pl.BlockSpec(memory_space=pltpu.HBM)
DMA = pltpu.SemaphoreType.DMA


class Copies:
    def __init__(self):
        self.started = []

    def __call__(self, src, dst, send, recv, device):
        return pltpu.make_async_remote_copy(
            src_ref=src, dst_ref=dst, send_sem=send, recv_sem=recv, device_id=device, device_id_type=MESH
        )

    def start(self, copy):
        copy.start()
        self.started.append(copy)

    def finish(self):
        for copy in self.started:
            copy.wait_send()


def chain_kernel(rows, cols, counts, row_prev, row_last, col_prev, col_last):
    slots = row_prev.shape[0]
    live = counts[0, 0]
    for last in (row_last, col_last):
        for b in range(last.shape[0]):
            last[b] = slots
    for s in range(slots):
        for ids, prev, last in ((rows, row_prev, row_last), (cols, col_prev, col_last)):
            b = ids[0, 0, s]
            before = last[b]
            prev[s] = before
            last[b] = jnp.where(s < live, s, before)


def chains(rows, cols, counts, row_blocks, col_blocks):
    slots = rows.shape[-1]
    return pl.pallas_call(
        chain_kernel,
        out_shape=tuple(jax.ShapeDtypeStruct((n,), jnp.int32) for n in (slots, row_blocks, slots, col_blocks)),
        in_specs=[SMEM] * 3,
        out_specs=(SMEM,) * 4,
    )(rows, cols, counts)


def layer_kernel(
    scale,
    row_prev, row_last, col_prev, col_last, rows, cols,
    feats_h, vals_h, dst_h, cot_h, w_self_h, w_neigh_h,
    out, w_out, source,
    feats, vals, dst, cot, w_self, w_neigh, sums, grads,
    c_send, got_c, x_send, got_x, z_send, got_z,
    h_send, got_h, y_send, got_y,
    w_full, w_c, w_xs, w_x, w_zs, w_z, w_mine, w_rows,
    load_sem,
    c_s, c_r, x_s, x_r, z_s, z_r, h_s, h_r, y_s, y_r,
    gz_s, gz_r, gx_s, gx_r, gc_s, gc_r,
    wc_s, wc_r, wx_s, wx_r, wz_s, wz_r, wr_s, wr_r, wg_s, wg_r, wl_s, wl_r,
):
    remote = Copies()
    row, col = lax.axis_index("row"), lax.axis_index("col")
    z, x, k = col // 4, (col // 2) % 2, col % 2
    y, h = row // 2, row % 2
    slots = vals.shape[0]
    quarter = slots // 4

    def at_col(zz, xx, kk):
        return (row, (zz % N) * 4 + xx * 2 + kk)

    def at_row(yy, hh):
        return ((yy % N) * 2 + hh, col)

    sibling, beside, across = at_col(z, x, 1 - k), at_col(z, 1 - x, k), at_row(y, 1 - h)

    def near(i):
        return at_col(z + i % N, (x + i // N) % 2, k)

    def far(i):
        return at_row(y + i % N, (h + i // N) % 2)

    barrier = pltpu.get_barrier_semaphore()

    def wz_copy(d):
        ref = w_zs.at[(z + d) % N]
        return remote(ref, w_z.at[z], wz_s.at[d], wz_r.at[d], near(d))

    def greet(i, c):
        pl.semaphore_signal(barrier, inc=1, device_id=near(i), device_id_type=MESH)
        pl.semaphore_signal(barrier, inc=1, device_id=far(i), device_id_type=MESH)
        return c

    pl.semaphore_signal(barrier, inc=1, device_id=sibling, device_id_type=MESH)
    lax.fori_loop(1, 2 * N, greet, 0)

    loads = [pltpu.make_async_copy(feats_h, feats, load_sem.at[0])]
    for i in range(4):
        part = pl.ds(i * quarter, quarter)
        loads.append(pltpu.make_async_copy(vals_h.at[part], vals.at[part], load_sem.at[1 + i]))
    for i, (src, dest) in enumerate(((dst_h, dst), (w_self_h, w_self), (w_neigh_h, w_neigh), (cot_h, cot))):
        loads.append(pltpu.make_async_copy(src, dest, load_sem.at[5 + i]))
    for load in loads:
        load.start()

    sums[slots] = jnp.zeros_like(sums[slots])
    loads[0].wait()
    for s in range(slots):
        if s % quarter == 0:
            loads[1 + s // quarter].wait()
        sums[s] = sums[row_prev[s]] + jnp.dot(vals[s], feats[cols[0, 0, s]], preferred_element_type=F32)

    def partial(zz, xx, kk):
        return sums[row_last[(zz % N) * 4 + xx * 2 + kk]]

    pl.semaphore_wait(barrier, 4 * N - 1)

    def c_copy(i):
        return remote(c_send.at[i], got_c.at[i], c_s.at[i], c_r.at[i], sibling)

    for i in range(2 * N):
        c_send[i] = partial(z + OFFSETS[i % N], 1 - x if i < N else x, 1 - k).astype(BF16)
        remote.start(c_copy(i))

    def x_copy(i):
        return remote(x_send.at[i], got_x.at[i], x_s.at[i], x_r.at[i], beside)

    for i in range(N):
        own = partial(z + OFFSETS[i], 1 - x, k)
        c_copy(i).wait_recv()
        x_send[i] = (own + got_c[i].astype(F32)).astype(BF16)
        remote.start(x_copy(i))

    for load in loads[5:]:
        load.wait()
    pre_self = jnp.dot(dst[...], w_self[...], preferred_element_type=F32)

    def col_piece(i):
        own = partial(z + OFFSETS[i], x, k)
        c_copy(N + i).wait_recv()
        own += got_c[N + i].astype(F32)
        x_copy(i).wait_recv()
        return own + got_x[i].astype(F32)

    def z_copy(i):
        return remote(z_send.at[i], got_z.at[i], z_s.at[i], z_r.at[i], at_col(z + OFFSETS[i], x, k))

    for i in range(N - 1):
        z_send[i] = col_piece(i).astype(BF16)
        remote.start(z_copy(i))
    total = col_piece(N - 1)
    for i in range(N - 1):
        z_copy(i).wait_recv()
        total += got_z[i].astype(F32)
    agg = total.astype(BF16)

    pre = pre_self + jnp.dot(agg, w_neigh[...], preferred_element_type=F32)
    sig = jax.nn.sigmoid(pre)
    gpre = (cot[...].astype(F32) * sig * (1.0 + pre * (1.0 - sig))).astype(BF16)
    mine = k * 2 * N + x * N
    me = mine + z
    grads[me] = lax.dot_general(
        gpre, w_neigh[...], (((1,), (1,)), ((), ())), preferred_element_type=F32
    ).astype(BF16)

    def gz_copy(i):
        ref = grads.at[me]
        return remote(ref, ref, gz_s.at[i], gz_r.at[i], at_col(z + SPREAD[i], x, k))

    def gx_copy(off):
        ref = grads.at[mine + (z + N - off) % N]
        return remote(ref, ref, gx_s.at[off], gx_r.at[off], beside)

    def gc_copy(other, off):
        ref = grads.at[k * 2 * N + ((x + other) % 2) * N + (z + N - off) % N]
        return remote(ref, ref, gc_s.at[other * N + off], gc_r.at[other * N + off], sibling)

    for i in range(N - 1):
        remote.start(gz_copy(i))
    remote.start(gx_copy(0))
    remote.start(gc_copy(0, 0))
    out[...] = (pre * sig).astype(BF16)

    feat = dst.shape[1]
    pieces, wide, hid = w_full.shape
    half = pieces // 2
    for base, left in ((0, dst[...]), (1, agg)):
        dw = lax.dot_general(left, gpre, (((0,), (0,)), ((), ())), preferred_element_type=F32)
        w_full[pl.ds(base * half, half)] = dw.reshape(half, wide, hid)
    wc_copy = remote(w_full.at[pl.ds((1 - k) * half, half)], w_c, wc_s, wc_r, sibling)
    wx_copy = remote(w_xs, w_x, wx_s, wx_r, beside)
    remote.start(wc_copy)

    def from_beside(off):
        gx_copy(off).wait_recv()
        remote.start(gc_copy(1, off))

    for i, off in enumerate(SPREAD):
        gz_copy(i).wait_recv()
        remote.start(gx_copy(off))
        remote.start(gc_copy(0, off))
        if i == 1:
            wc_copy.wait_recv()
            w_xs[...] = w_full[pl.ds(k * half + (1 - x) * N, N)] + w_c[pl.ds((1 - x) * N, N)]
            remote.start(wx_copy)
        if i == 3:
            from_beside(0)
    for i, off in enumerate(SPREAD):
        from_beside(off)
        if i == 3:
            wx_copy.wait_recv()
            w_zs[...] = w_full[pl.ds(k * half + x * N, N)] + w_c[pl.ds(x * N, N)] + w_x[...]
            for d in range(1, N):
                remote.start(wz_copy(d))
    for i in range(2 * N):
        gc_copy(i // N, i % N).wait_recv()

    for s in range(slots):
        r = rows[0, 0, s]
        g = grads[(r % 2) * 2 * N + ((r // 2) % 2) * N + r // 4]
        sums[s] = sums[col_prev[s]] + lax.dot_general(
            vals[s], g, (((0,), (0,)), ((), ())), preferred_element_type=F32
        )

    def source_partial(yy, hh):
        return sums[col_last[(yy % N) * 2 + hh]]

    def h_copy(i):
        return remote(h_send.at[i], got_h.at[i], h_s.at[i], h_r.at[i], across)

    for i in range(N):
        h_send[i] = source_partial(y + OFFSETS[i], 1 - h).astype(BF16)
        remote.start(h_copy(i))

    total = w_zs[z]
    for d in range(1, N):
        wz_copy(d).wait_recv()
        total += w_z[(z + N - d) % N]
    w_mine[...] = total
    w_rows[row] = total

    def wr_copy(i):
        return remote(w_mine, w_rows.at[row], wr_s.at[i], wr_r.at[i], far(i))

    for i in range(1, 2 * N):
        remote.start(wr_copy(i))

    def y_copy(i):
        return remote(y_send.at[i], got_y.at[i], y_s.at[i], y_r.at[i], at_row(y + OFFSETS[i], h))

    def row_piece(i):
        own = source_partial(y + OFFSETS[i], h)
        h_copy(i).wait_recv()
        return own + got_h[i].astype(F32)

    for i in range(N - 1):
        y_send[i] = row_piece(i).astype(BF16)
        remote.start(y_copy(i))

    for i in range(1, 2 * N):
        wr_copy(i).wait_recv()
    total = w_rows[0]
    for i in range(1, 2 * N):
        total += w_rows[i]
    w_out[me] = total * scale

    def wg_copy(i):
        return remote(w_out.at[me], w_out.at[me], wg_s.at[i], wg_r.at[i], near(i))

    for i in range(1, 2 * N):
        remote.start(wg_copy(i))

    total = row_piece(N - 1)
    for i in range(N - 1):
        y_copy(i).wait_recv()
        total += got_y[i].astype(F32)
    source[...] = total

    for i in range(1, 2 * N):
        wg_copy(i).wait_recv()
    ref = w_out.at[pl.ds(k * half, half)]
    wl_copy = remote(ref, ref, wl_s, wl_r, sibling)
    remote.start(wl_copy)
    wl_copy.wait_recv()
    remote.finish()


def layer(scale, tables, rows, cols, feats, vals, dst, cot, w_self, w_neigh):
    slots, block, _ = vals.shape
    width = feats.shape[-1]
    hid = w_self.shape[1]
    wide = 2 * width // (4 * N)

    def blocks(n, kind=BF16):
        return pltpu.VMEM((n, block, width), kind)

    def slabs(n):
        return pltpu.VMEM((n, wide, hid), F32)

    return pl.pallas_call(
        functools.partial(layer_kernel, scale),
        out_shape=(
            jax.ShapeDtypeStruct((block, hid), BF16),
            jax.ShapeDtypeStruct((4 * N, wide, hid), F32),
            jax.ShapeDtypeStruct((block, width), F32),
        ),
        in_specs=[SMEM] * 6 + [HBM] * 6,
        out_specs=(VMEM,) * 3,
        scratch_shapes=[
            blocks(feats.shape[0]), pltpu.VMEM(vals.shape, BF16), pltpu.VMEM(dst.shape, BF16),
            pltpu.VMEM(cot.shape, BF16), pltpu.VMEM(w_self.shape, BF16), pltpu.VMEM(w_neigh.shape, BF16),
            blocks(slots + 1, F32), blocks(4 * N),
            blocks(2 * N), blocks(2 * N), blocks(N), blocks(N), blocks(N - 1), blocks(N - 1),
            blocks(N), blocks(N), blocks(N - 1), blocks(N - 1),
            slabs(4 * N), slabs(2 * N), slabs(N), slabs(N), slabs(N), slabs(N),
            pltpu.VMEM((wide, hid), F32), slabs(2 * N),
            DMA((9,)),
            DMA((2 * N,)), DMA((2 * N,)), DMA((N,)), DMA((N,)), DMA((N,)), DMA((N,)),
            DMA((N,)), DMA((N,)), DMA((N,)), DMA((N,)),
            DMA((N,)), DMA((N,)), DMA((N,)), DMA((N,)), DMA((2 * N,)), DMA((2 * N,)),
            DMA, DMA, DMA, DMA, DMA((N,)), DMA((N,)), DMA((2 * N,)), DMA((2 * N,)), DMA((2 * N,)), DMA((2 * N,)),
            DMA, DMA,
        ],
        compiler_params=pltpu.CompilerParams(
            collective_id=0, has_side_effects=True, vmem_limit_bytes=60 * 1024 * 1024
        ),
    )(*tables, rows, cols, feats, vals, dst, cot, w_self, w_neigh)


def per_device(features, dst_features, w_self, w_neigh, cotangent, block_values, block_rows, block_cols, block_counts):
    block = block_values.shape[-1]
    width = features.shape[-1]
    tables = chains(block_rows, block_cols, block_counts, 4 * N, 2 * N)
    nodes = dst_features.shape[0] * lax.axis_size("row") * lax.axis_size("col")
    out, w_all, source = layer(
        1.0 / math.sqrt(nodes), tables, block_rows, block_cols, features.reshape(-1, block, width),
        block_values[0, 0], dst_features, cotangent, w_self, w_neigh,
    )
    w_all = w_all.reshape(2, width, -1)
    return out, w_all[0], w_all[1], source[None]


def solution(mesh):
    placed = (
        P("col", None, None),
        P(("row", "col"), None),
        P(),
        P(),
        P(("row", "col"), None),
        P("row", "col", None, None, None),
        P("row", "col", None),
        P("row", "col", None),
        P("row", "col"),
    )
    return jax.shard_map(
        per_device,
        mesh=mesh,
        in_specs=placed,
        out_specs=(P(("row", "col"), None), P(), P(), P("col", "row", None)),
        check_vma=False,
    )
```

time: 83.7 us -> 70.5 us (0.84)
  Pallas kernels: 73.7 us -> 65.7 us
  local copies, waits for them, and re-layouts: 8.2 us -> 3.21 us
    pallas_call x1, Pallas kernels: 72.3 us -> 64.3 us  [layer(): pl.pallas_call(functools.partial(layer_kernel, scale), out_shape=(jax.Sha...]
    unnamed x26 -> x6, local copies, waits for them, and re-layouts: 7.48 us -> 1.5 us
    squeeze x1, local copies, waits for them, and re-layouts: 0.72 us -> 1.72 us  [per_device(): return (out, w_all[0], w_all[1], source[None])]
where the time goes in v3:
time: 70.5 us; the launch traced here: 70.3 us
  Pallas kernels  65.7 us (93%)
  local copies, waits for them, and re-layouts  3.21 us (5%)
  between operations  1.3 us (2%)
    pallas_call x1, Pallas kernels, layer(): pl.pallas_call(functools.partial(layer_kernel, scale), out_shape=(jax.Sha...  64.3 us
    squeeze x1, local copies, waits for them, and re-layouts, per_device(): return (out, w_all[0], w_all[1], source[None])  1.72 us
    unnamed x6, local copies, waits for them, and re-layouts  1.5 us
    pallas_call x1, Pallas kernels, chains(): pl.pallas_call(chain_kernel, out_shape=tuple((jax.ShapeDtypeStruct((n,),...  1.41 us

profile of v3, /device:TPU:1, one launch (start us, length us, event | category | flops | bytes accessed | tf_op | source)
XLA Modules:
  0.0 70.3 jit_solution(5064601009375072712)
XLA Ops:
  1.3 1.4 %shard_map.120 = (s32[32]{0:T(128)}, s32[32]{0:T(128)}, s32[32]{0:T(128)}, s32[16]{0:T(128)}) custom-call(s32[1,1,32]{2,1,0:T(1,128)} %rows.3, s32[1,1,32]{2,1,0:T(1,128)} %cols.3, s32[1,1]{1,0:T(1,128)S(6)} %copy.15.counts), custom_call_target="tpu_custom_call" | custom-call | tf_op jit(solution)/shard_map/pallas_call | solution.py:57
  2.7 64.3 %shard_map.121 = (bf16[128,256]{1,0:T(8,128)(2,1)}, f32[32,8,256]{2,1,0:T(8,128)}, f32[128,128]{1,0:T(8,128)}) custom-call(s32[32]{0:T(128)} %get-tuple-element.11.row_prev, s32[32]{0:T(128)} %get-tuple-element.12.row_last, s32[32]{0:T(128)} %get-tuple-element.13.col_prev, s32[16]{0:T(128)} %get-tuple-element.14.col_last, s32[1,1,32]{2,1,0:T(1,128)} %rows.3, ...), custom_call_target="tpu_custom_call" | custom-call | tf_op jit(solution)/shard_map/pallas_call | solution.py:317
  67.0 0.0 copy-start.1
  67.0 1.7 %slice_bitcast_fusion = (f32[128,256]{1,0:T(8,128)}, f32[128,256]{1,0:T(8,128)}) fusion(f32[32,8,256]{2,1,0:T(8,128)} %get-tuple-element.16), kind=kLoop, calls=%fused_computation | loop fusion | bytes 524288 | tf_op jit(solution)/shard_map/squeeze | solution.py:357
  68.8 0.0 copy-done.1
  68.8 0.0 copy-start
  68.8 0.6 copy.16
  69.4 0.2 copy-done
  69.6 0.6 copy.17
Async XLA Ops:
  67.0 1.7 %copy-start.1 = (bf16[128,256]{1,0:T(8,128)(2,1)S(1)}, bf16[128,256]{1,0:T(8,128)(2,1)}, u32[]{:S(2)}) copy-start(bf16[128,256]{1,0:T(8,128)(2,1)} %get-tuple-element.24) | copy-start | bytes 196612
  68.8 0.9 %copy-start = (f32[128,128]{1,0:T(8,128)S(1)}, f32[128,128]{1,0:T(8,128)}, u32[]{:S(2)}) copy-start(f32[128,128]{1,0:T(8,128)} %get-tuple-element.17) | copy-start | bytes 196612

commit v4 on v3

v4 whole, which is shorter than its diff:
```python
import functools
import math

import jax
import jax.numpy as jnp
from jax import lax
from jax.experimental import pallas as pl
from jax.experimental.pallas import tpu as pltpu
from jax.sharding import PartitionSpec as P

BF16 = jnp.bfloat16
F32 = jnp.float32
MESH = pl.DeviceIdType.MESH
N = 8
OFFSETS = (4, 3, 5, 2, 6, 1, 7, 0)
SPREAD = (1, 7, 2, 6, 3, 5, 4)
SMEM = pl.BlockSpec(memory_space=pltpu.SMEM)
HBM = pl.BlockSpec(memory_space=pltpu.HBM)
DMA = pltpu.SemaphoreType.DMA


class Copies:
    def __init__(self):
        self.started = []

    def __call__(self, src, dst, send, recv, device):
        return pltpu.make_async_remote_copy(
            src_ref=src, dst_ref=dst, send_sem=send, recv_sem=recv, device_id=device, device_id_type=MESH
        )

    def start(self, copy):
        copy.start()
        self.started.append(copy)

    def finish(self):
        for copy in self.started:
            copy.wait_send()


def chain(ids, live):
    slots = ids.shape[1]
    t = lax.broadcasted_iota(jnp.int32, (slots, slots), 0)
    s = lax.broadcasted_iota(jnp.int32, (slots, slots), 1)
    along = jnp.broadcast_to(ids, (slots, slots))
    down = jnp.sum(jnp.where(t == s, along, 0), axis=1, keepdims=True)
    used = t < live
    prev = jnp.max(jnp.where((down == along) & (t < s) & used, t, -1), axis=0, keepdims=True)
    last = jnp.max(jnp.where((down == s) & used, t, -1), axis=0, keepdims=True)
    return jnp.where(prev < 0, slots, prev), jnp.where(last < 0, slots, last)


def layer_kernel(
    scale,
    rows_h, cols_h, counts, feats_h, vals_h, dst_h, cot_h, w_self_h, w_neigh_h,
    out_h, w_out_h, source_h,
    rows, cols, tables, table, out, w_out, source, feats, vals, dst, cot, w_self, w_neigh, sums, grads,
    c_send, got_c, x_send, got_x, z_send, got_z,
    h_send, got_h, y_send, got_y,
    w_full, w_c, w_xs, w_x, w_zs, w_z, w_mine, w_rows,
    load_sem, table_sem, store_sem,
    c_s, c_r, x_s, x_r, z_s, z_r, h_s, h_r, y_s, y_r,
    gz_s, gz_r, gx_s, gx_r, gc_s, gc_r,
    wc_s, wc_r, wx_s, wx_r, wz_s, wz_r, wr_s, wr_r, wg_s, wg_r, wl_s, wl_r,
):
    remote = Copies()
    row, col = lax.axis_index("row"), lax.axis_index("col")
    z, x, k = col // 4, (col // 2) % 2, col % 2
    y, h = row // 2, row % 2
    slots = vals.shape[0]
    quarter = slots // 4

    def at_col(zz, xx, kk):
        return (row, (zz % N) * 4 + xx * 2 + kk)

    def at_row(yy, hh):
        return ((yy % N) * 2 + hh, col)

    mine = k * 2 * N + x * N
    me = mine + z
    sibling, beside, across = at_col(z, x, 1 - k), at_col(z, 1 - x, k), at_row(y, 1 - h)

    def near(i):
        return at_col(z + i % N, (x + i // N) % 2, k)

    def far(i):
        return at_row(y + i % N, (h + i // N) % 2)

    barrier = pltpu.get_barrier_semaphore()

    def wz_copy(d):
        ref = w_zs.at[(z + d) % N]
        return remote(ref, w_z.at[z], wz_s.at[d], wz_r.at[d], near(d))

    def wr_copy(i):
        return remote(w_mine, w_rows.at[row], wr_s.at[i], wr_r.at[i], far(i))

    def wg_copy(i):
        return remote(w_out.at[me], w_out.at[me], wg_s.at[i], wg_r.at[i], near(i))

    def greet(i, c):
        pl.semaphore_signal(barrier, inc=1, device_id=near(i), device_id_type=MESH)
        pl.semaphore_signal(barrier, inc=1, device_id=far(i), device_id_type=MESH)
        return c

    pl.semaphore_signal(barrier, inc=1, device_id=sibling, device_id_type=MESH)
    lax.fori_loop(1, 2 * N, greet, 0)

    loads = []
    for i, (src, dest) in enumerate(((rows_h, rows), (cols_h, cols), (feats_h, feats))):
        loads.append(pltpu.make_async_copy(src, dest, load_sem.at[i]))
    for i in range(4):
        part = pl.ds(i * quarter, quarter)
        loads.append(pltpu.make_async_copy(vals_h.at[part], vals.at[part], load_sem.at[3 + i]))
    for i, (src, dest) in enumerate(((dst_h, dst), (w_self_h, w_self), (w_neigh_h, w_neigh), (cot_h, cot))):
        loads.append(pltpu.make_async_copy(src, dest, load_sem.at[7 + i]))
    for load in loads:
        load.start()

    sums[slots] = jnp.zeros_like(sums[slots])
    tables[...] = jnp.zeros_like(tables)
    for load in loads[:2]:
        load.wait()
    r, c = rows[...], cols[...]
    row_prev, row_last = chain(r, counts[0, 0])
    col_prev, col_last = chain(c, counts[0, 0])
    at = (r % 2) * (2 * N) + ((r // 2) % 2) * N + r // 4
    for i, line in enumerate((row_prev, row_last, col_prev, col_last, c, at)):
        tables[pl.ds(i, 1), pl.ds(0, slots)] = line
    to_scalars = pltpu.make_async_copy(tables, table, table_sem)
    to_scalars.start()
    to_scalars.wait()

    loads[2].wait()
    for s in range(slots):
        if s % quarter == 0:
            loads[3 + s // quarter].wait()
        sums[s] = sums[table[0, s]] + jnp.dot(vals[s], feats[table[4, s]], preferred_element_type=F32)

    def partial(zz, xx, kk):
        return sums[table[1, (zz % N) * 4 + xx * 2 + kk]]

    pl.semaphore_wait(barrier, 4 * N - 1)

    def c_copy(i):
        return remote(c_send.at[i], got_c.at[i], c_s.at[i], c_r.at[i], sibling)

    for i in range(2 * N):
        c_send[i] = partial(z + OFFSETS[i % N], 1 - x if i < N else x, 1 - k).astype(BF16)
        remote.start(c_copy(i))

    def x_copy(i):
        return remote(x_send.at[i], got_x.at[i], x_s.at[i], x_r.at[i], beside)

    for i in range(N):
        own = partial(z + OFFSETS[i], 1 - x, k)
        c_copy(i).wait_recv()
        x_send[i] = (own + got_c[i].astype(F32)).astype(BF16)
        remote.start(x_copy(i))

    for load in loads[7:]:
        load.wait()
    pre_self = jnp.dot(dst[...], w_self[...], preferred_element_type=F32)

    def col_piece(i):
        own = partial(z + OFFSETS[i], x, k)
        c_copy(N + i).wait_recv()
        own += got_c[N + i].astype(F32)
        x_copy(i).wait_recv()
        return own + got_x[i].astype(F32)

    def z_copy(i):
        return remote(z_send.at[i], got_z.at[i], z_s.at[i], z_r.at[i], at_col(z + OFFSETS[i], x, k))

    for i in range(N - 1):
        z_send[i] = col_piece(i).astype(BF16)
        remote.start(z_copy(i))
    total = col_piece(N - 1)
    for i in range(N - 1):
        z_copy(i).wait_recv()
        total += got_z[i].astype(F32)
    agg = total.astype(BF16)

    pre = pre_self + jnp.dot(agg, w_neigh[...], preferred_element_type=F32)
    sig = jax.nn.sigmoid(pre)
    gpre = (cot[...].astype(F32) * sig * (1.0 + pre * (1.0 - sig))).astype(BF16)
    grads[me] = lax.dot_general(
        gpre, w_neigh[...], (((1,), (1,)), ((), ())), preferred_element_type=F32
    ).astype(BF16)

    def gz_copy(i):
        ref = grads.at[me]
        return remote(ref, ref, gz_s.at[i], gz_r.at[i], at_col(z + SPREAD[i], x, k))

    def gx_copy(off):
        ref = grads.at[mine + (z + N - off) % N]
        return remote(ref, ref, gx_s.at[off], gx_r.at[off], beside)

    def gc_copy(other, off):
        ref = grads.at[k * 2 * N + ((x + other) % 2) * N + (z + N - off) % N]
        return remote(ref, ref, gc_s.at[other * N + off], gc_r.at[other * N + off], sibling)

    for i in range(N - 1):
        remote.start(gz_copy(i))
    remote.start(gx_copy(0))
    remote.start(gc_copy(0, 0))
    out[...] = (pre * sig).astype(BF16)
    stores = [pltpu.make_async_copy(out, out_h, store_sem.at[0])]
    stores[0].start()

    feat = dst.shape[1]
    pieces, wide, hid = w_full.shape
    half = pieces // 2
    for base, left in ((0, dst[...]), (1, agg)):
        dw = lax.dot_general(left, gpre, (((0,), (0,)), ((), ())), preferred_element_type=F32)
        w_full[pl.ds(base * half, half)] = dw.reshape(half, wide, hid)
    wc_copy = remote(w_full.at[pl.ds((1 - k) * half, half)], w_c, wc_s, wc_r, sibling)
    wx_copy = remote(w_xs, w_x, wx_s, wx_r, beside)
    remote.start(wc_copy)

    def from_beside(off):
        gx_copy(off).wait_recv()
        remote.start(gc_copy(1, off))

    wc_copy.wait_recv()
    w_xs[...] = w_full[pl.ds(k * half + (1 - x) * N, N)] + w_c[pl.ds((1 - x) * N, N)]
    remote.start(wx_copy)
    for i, off in enumerate(SPREAD):
        gz_copy(i).wait_recv()
        remote.start(gx_copy(off))
        remote.start(gc_copy(0, off))
        if i == 3:
            from_beside(0)
            wx_copy.wait_recv()
            w_zs[...] = w_full[pl.ds(k * half + x * N, N)] + w_c[pl.ds(x * N, N)] + w_x[...]
            for d in range(1, N):
                remote.start(wz_copy(d))
    for off in SPREAD:
        from_beside(off)

    total = w_zs[z]
    for d in range(1, N):
        wz_copy(d).wait_recv()
        total += w_z[(z + N - d) % N]
    w_mine[...] = total
    w_rows[row] = total
    for i in range(1, 2 * N):
        remote.start(wr_copy(i))
    for i in range(2 * N):
        gc_copy(i // N, i % N).wait_recv()

    for s in range(slots):
        sums[s] = sums[table[2, s]] + lax.dot_general(
            vals[s], grads[table[5, s]], (((0,), (0,)), ((), ())), preferred_element_type=F32
        )

    def source_partial(yy, hh):
        return sums[table[3, (yy % N) * 2 + hh]]

    def h_copy(i):
        return remote(h_send.at[i], got_h.at[i], h_s.at[i], h_r.at[i], across)

    for i in range(N):
        h_send[i] = source_partial(y + OFFSETS[i], 1 - h).astype(BF16)
        remote.start(h_copy(i))

    for i in range(1, 2 * N):
        wr_copy(i).wait_recv()
    total = w_rows[0]
    for i in range(1, 2 * N):
        total += w_rows[i]
    w_out[me] = total * scale
    for i in range(1, 2 * N):
        remote.start(wg_copy(i))

    def y_copy(i):
        return remote(y_send.at[i], got_y.at[i], y_s.at[i], y_r.at[i], at_row(y + OFFSETS[i], h))

    def row_piece(i):
        own = source_partial(y + OFFSETS[i], h)
        h_copy(i).wait_recv()
        return own + got_h[i].astype(F32)

    for i in range(N - 1):
        y_send[i] = row_piece(i).astype(BF16)
        remote.start(y_copy(i))

    total = row_piece(N - 1)
    for i in range(N - 1):
        y_copy(i).wait_recv()
        total += got_y[i].astype(F32)
    source[...] = total
    stores.append(pltpu.make_async_copy(source, source_h, store_sem.at[1]))
    stores[1].start()

    for i in range(1, 2 * N):
        wg_copy(i).wait_recv()
    ref = w_out.at[pl.ds(k * half, half)]
    wl_copy = remote(ref, ref, wl_s, wl_r, sibling)
    remote.start(wl_copy)
    wl_copy.wait_recv()
    stores.append(pltpu.make_async_copy(w_out, w_out_h, store_sem.at[2]))
    stores[2].start()
    remote.finish()
    for store in stores:
        store.wait()


def layer(scale, rows, cols, counts, feats, vals, dst, cot, w_self, w_neigh):
    slots, block, _ = vals.shape
    width = feats.shape[-1]
    hid = w_self.shape[1]
    wide = 2 * width // (4 * N)
    results = (
        jax.ShapeDtypeStruct((block, hid), BF16),
        jax.ShapeDtypeStruct((4 * N, wide, hid), F32),
        jax.ShapeDtypeStruct((block, width), F32),
    )

    def like(a):
        return pltpu.VMEM(a.shape, a.dtype)

    def blocks(n, kind=BF16):
        return pltpu.VMEM((n, block, width), kind)

    def slabs(n):
        return pltpu.VMEM((n, wide, hid), F32)

    return pl.pallas_call(
        functools.partial(layer_kernel, scale),
        out_shape=results,
        in_specs=[HBM, HBM, SMEM] + [HBM] * 6,
        out_specs=(HBM,) * 3,
        scratch_shapes=[
            like(rows), like(cols), pltpu.VMEM((8, 128), jnp.int32), pltpu.SMEM((8, 128), jnp.int32),
            *map(like, results), like(feats), like(vals), like(dst), like(cot), like(w_self), like(w_neigh),
            blocks(slots + 1, F32), blocks(4 * N),
            blocks(2 * N), blocks(2 * N), blocks(N), blocks(N), blocks(N - 1), blocks(N - 1),
            blocks(N), blocks(N), blocks(N - 1), blocks(N - 1),
            slabs(4 * N), slabs(2 * N), slabs(N), slabs(N), slabs(N), slabs(N),
            pltpu.VMEM((wide, hid), F32), slabs(2 * N),
            DMA((11,)), DMA, DMA((3,)),
            DMA((2 * N,)), DMA((2 * N,)), DMA((N,)), DMA((N,)), DMA((N,)), DMA((N,)),
            DMA((N,)), DMA((N,)), DMA((N,)), DMA((N,)),
            DMA((N,)), DMA((N,)), DMA((N,)), DMA((N,)), DMA((2 * N,)), DMA((2 * N,)),
            DMA, DMA, DMA, DMA, DMA((N,)), DMA((N,)), DMA((2 * N,)), DMA((2 * N,)), DMA((2 * N,)), DMA((2 * N,)),
            DMA, DMA,
        ],
        compiler_params=pltpu.CompilerParams(
            collective_id=0, has_side_effects=True, vmem_limit_bytes=60 * 1024 * 1024
        ),
    )(rows, cols, counts, feats, vals, dst, cot, w_self, w_neigh)


def hand_kernel(out_h, w_h, source_h, out, w_self, w_neigh, source, sem):
    half = w_self.shape[0]
    pairs = (
        (out_h, out), (w_h.at[pl.ds(0, half)], w_self), (w_h.at[pl.ds(half, half)], w_neigh), (source_h, source)
    )
    copies = [pltpu.make_async_copy(src, dest, sem.at[i]) for i, (src, dest) in enumerate(pairs)]
    for copy in copies:
        copy.start()
    for copy in copies:
        copy.wait()


def hand(out, w_all, source):
    pieces, wide, hid = w_all.shape
    grad = jax.ShapeDtypeStruct((pieces // 2, wide, hid), F32)
    return pl.pallas_call(
        hand_kernel,
        out_shape=(jax.ShapeDtypeStruct(out.shape, BF16), grad, grad, jax.ShapeDtypeStruct(source.shape, F32)),
        in_specs=[HBM] * 3,
        out_specs=(HBM,) * 4,
        scratch_shapes=[DMA((4,))],
        compiler_params=pltpu.CompilerParams(vmem_limit_bytes=60 * 1024 * 1024),
    )(out, w_all, source)


def per_device(features, dst_features, w_self, w_neigh, cotangent, block_values, block_rows, block_cols, block_counts):
    block = block_values.shape[-1]
    width = features.shape[-1]
    nodes = dst_features.shape[0] * lax.axis_size("row") * lax.axis_size("col")
    results = layer(
        1.0 / math.sqrt(nodes), block_rows[0], block_cols[0], block_counts, features.reshape(-1, block, width),
        block_values[0, 0], dst_features, cotangent, w_self, w_neigh,
    )
    out, grad_self, grad_neigh, source = hand(*results)
    return out, grad_self.reshape(width, -1), grad_neigh.reshape(width, -1), source[None]


def solution(mesh):
    placed = (
        P("col", None, None),
        P(("row", "col"), None),
        P(),
        P(),
        P(("row", "col"), None),
        P("row", "col", None, None, None),
        P("row", "col", None),
        P("row", "col", None),
        P("row", "col"),
    )
    return jax.shard_map(
        per_device,
        mesh=mesh,
        in_specs=placed,
        out_specs=(P(("row", "col"), None), P(), P(), P("col", "row", None)),
        check_vma=False,
    )
```

time: 70.5 us -> 74.7 us (1.060)
  Pallas kernels: 65.7 us -> 73.2 us
  local copies, waits for them, and re-layouts: 3.21 us -> 0 us
    pallas_call x2, Pallas kernels: 65.7 us -> 73.2 us  [the longest x1 60.2 us: layer(): pl.pallas_call(functools.partial(layer_kernel, scale), out_shape=results,...]
    squeeze x1 -> x0, local copies, waits for them, and re-layouts: 1.72 us -> none  [per_device(): return (out, w_all[0], w_all[1], source[None])]
    unnamed x6 -> x0, local copies, waits for them, and re-layouts: 1.5 us -> none
where the time goes in v4:
time: 74.7 us; the launch traced here: 74.5 us
  Pallas kernels  73.2 us (98%)
  between operations  1.29 us (2%)
    pallas_call x1, Pallas kernels, layer(): pl.pallas_call(functools.partial(layer_kernel, scale), out_shape=results,...  60.2 us
    pallas_call x1, Pallas kernels, hand(): pl.pallas_call(hand_kernel, out_shape=(jax.ShapeDtypeStruct(out.shape, BF...  13.1 us

profile of v4, /device:TPU:1, one launch (start us, length us, event | category | flops | bytes accessed | tf_op | source)
XLA Modules:
  0.0 74.5 jit_solution(2825219220201645414)
XLA Ops:
  1.3 60.2 %shard_map.120 = (bf16[128,256]{1,0:T(8,128)(2,1)}, f32[32,8,256]{2,1,0:T(8,128)}, f32[128,128]{1,0:T(8,128)}) custom-call(s32[1,32]{1,0:T(1,128)} %bitcast.9, s32[1,32]{1,0:T(1,128)} %bitcast.10, s32[1,1]{1,0:T(1,128)S(6)} %copy.13.counts, bf16[16,128,128]{2,1,0:T(8,128)(2,1)} %bitcast.8, bf16[32,128,128]{2,1,0:T(8,128)(2,1)} %bitcast.7, ...), custom_call_target="tpu_custom_call" | custom-call | tf_op jit(solution)/shard_map/pallas_call | solution.py:328
  61.5 13.1 %shard_map.121 = (bf16[128,256]{1,0:T(8,128)(2,1)}, f32[16,8,256]{2,1,0:T(8,128)}, f32[16,8,256]{2,1,0:T(8,128)}, f32[128,128]{1,0:T(8,128)}) custom-call(bf16[128,256]{1,0:T(8,128)(2,1)} %get-tuple-element.11.out_h, f32[32,8,256]{2,1,0:T(8,128)} %get-tuple-element.12.w_h, f32[128,128]{1,0:T(8,128)} %get-tuple-element.13.source_h), custom_call_target="tpu_custom_call" | custom-call | tf_op jit(solution)/shard_map/pallas_call | solution.py:369

commit v5 on v4

--- a/solution.py
+++ b/solution.py
@@ -56,11 +56,11 @@
     rows, cols, tables, table, out, w_out, source, feats, vals, dst, cot, w_self, w_neigh, sums, grads,
     c_send, got_c, x_send, got_x, z_send, got_z,
     h_send, got_h, y_send, got_y,
-    w_full, w_c, w_xs, w_x, w_zs, w_z, w_mine, w_rows,
+    w_full, w_c, w_half, w_send, got_w, w_mine, w_rows,
     load_sem, table_sem, store_sem,
     c_s, c_r, x_s, x_r, z_s, z_r, h_s, h_r, y_s, y_r,
     gz_s, gz_r, gx_s, gx_r, gc_s, gc_r,
-    wc_s, wc_r, wx_s, wx_r, wz_s, wz_r, wr_s, wr_r, wg_s, wg_r, wl_s, wl_r,
+    wc_s, wc_r, wz_s, wz_r, wr_s, wr_r, wg_s, wg_r, wl_s, wl_r,
 ):
     remote = Copies()
     row, col = lax.axis_index("row"), lax.axis_index("col")
@@ -87,9 +87,9 @@
 
     barrier = pltpu.get_barrier_semaphore()
 
-    def wz_copy(d):
-        ref = w_zs.at[(z + d) % N]
-        return remote(ref, w_z.at[z], wz_s.at[d], wz_r.at[d], near(d))
+    def wz_copy(i):
+        ref = w_send.at[((x + i // N) % 2) * N + (z + i) % N]
+        return remote(ref, got_w.at[i], wz_s.at[i], wz_r.at[i], near(i))
 
     def wr_copy(i):
         return remote(w_mine, w_rows.at[row], wr_s.at[i], wr_r.at[i], far(i))
@@ -214,7 +214,6 @@
         dw = lax.dot_general(left, gpre, (((0,), (0,)), ((), ())), preferred_element_type=F32)
         w_full[pl.ds(base * half, half)] = dw.reshape(half, wide, hid)
     wc_copy = remote(w_full.at[pl.ds((1 - k) * half, half)], w_c, wc_s, wc_r, sibling)
-    wx_copy = remote(w_xs, w_x, wx_s, wx_r, beside)
     remote.start(wc_copy)
 
     def from_beside(off):
@@ -222,29 +221,27 @@
         remote.start(gc_copy(1, off))
 
     wc_copy.wait_recv()
-    w_xs[...] = w_full[pl.ds(k * half + (1 - x) * N, N)] + w_c[pl.ds((1 - x) * N, N)]
-    remote.start(wx_copy)
+    w_half[...] = w_full[pl.ds(k * half, half)] + w_c[...]
+    w_send[...] = w_half[...].astype(BF16)
+    for i in range(1, 2 * N):
+        remote.start(wz_copy(i))
     for i, off in enumerate(SPREAD):
         gz_copy(i).wait_recv()
         remote.start(gx_copy(off))
         remote.start(gc_copy(0, off))
         if i == 3:
             from_beside(0)
-            wx_copy.wait_recv()
-            w_zs[...] = w_full[pl.ds(k * half + x * N, N)] + w_c[pl.ds(x * N, N)] + w_x[...]
-            for d in range(1, N):
-                remote.start(wz_copy(d))
+
+    total = w_half[x * N + z]
+    for i in range(1, 2 * N):
+        wz_copy(i).wait_recv()
+        total += got_w[i].astype(F32)
+    w_mine[...] = total
+    w_rows[row] = total
+    for i in range(1, 2 * N):
+        remote.start(wr_copy(i))
     for off in SPREAD:
         from_beside(off)
-
-    total = w_zs[z]
-    for d in range(1, N):
-        wz_copy(d).wait_recv()
-        total += w_z[(z + N - d) % N]
-    w_mine[...] = total
-    w_rows[row] = total
-    for i in range(1, 2 * N):
-        remote.start(wr_copy(i))
     for i in range(2 * N):
         gc_copy(i // N, i % N).wait_recv()
 
@@ -283,6 +280,12 @@
     for i in range(N - 1):
         y_send[i] = row_piece(i).astype(BF16)
         remote.start(y_copy(i))
+
+    for i in range(1, 2 * N):
+        wg_copy(i).wait_recv()
+    ref = w_out.at[pl.ds(k * half, half)]
+    wl_copy = remote(ref, ref, wl_s, wl_r, sibling)
+    remote.start(wl_copy)
 
     total = row_piece(N - 1)
     for i in range(N - 1):
@@ -291,12 +294,6 @@
     source[...] = total
     stores.append(pltpu.make_async_copy(source, source_h, store_sem.at[1]))
     stores[1].start()
-
-    for i in range(1, 2 * N):
-        wg_copy(i).wait_recv()
-    ref = w_out.at[pl.ds(k * half, half)]
-    wl_copy = remote(ref, ref, wl_s, wl_r, sibling)
-    remote.start(wl_copy)
     wl_copy.wait_recv()
     stores.append(pltpu.make_async_copy(w_out, w_out_h, store_sem.at[2]))
     stores[2].start()
@@ -322,8 +319,8 @@
     def blocks(n, kind=BF16):
         return pltpu.VMEM((n, block, width), kind)
 
-    def slabs(n):
-        return pltpu.VMEM((n, wide, hid), F32)
+    def slabs(n, kind=F32):
+        return pltpu.VMEM((n, wide, hid), kind)
 
     return pl.pallas_call(
         functools.partial(layer_kernel, scale),
@@ -336,13 +333,13 @@
             blocks(slots + 1, F32), blocks(4 * N),
             blocks(2 * N), blocks(2 * N), blocks(N), blocks(N), blocks(N - 1), blocks(N - 1),
             blocks(N), blocks(N), blocks(N - 1), blocks(N - 1),
-            slabs(4 * N), slabs(2 * N), slabs(N), slabs(N), slabs(N), slabs(N),
+            slabs(4 * N), slabs(2 * N), slabs(2 * N), slabs(2 * N, BF16), slabs(2 * N, BF16),
             pltpu.VMEM((wide, hid), F32), slabs(2 * N),
             DMA((11,)), DMA, DMA((3,)),
             DMA((2 * N,)), DMA((2 * N,)), DMA((N,)), DMA((N,)), DMA((N,)), DMA((N,)),
             DMA((N,)), DMA((N,)), DMA((N,)), DMA((N,)),
             DMA((N,)), DMA((N,)), DMA((N,)), DMA((N,)), DMA((2 * N,)), DMA((2 * N,)),
-            DMA, DMA, DMA, DMA, DMA((N,)), DMA((N,)), DMA((2 * N,)), DMA((2 * N,)), DMA((2 * N,)), DMA((2 * N,)),
+            DMA, DMA, DMA((2 * N,)), DMA((2 * N,)), DMA((2 * N,)), DMA((2 * N,)), DMA((2 * N,)), DMA((2 * N,)),
             DMA, DMA,
         ],
         compiler_params=pltpu.CompilerParams(
@@ -351,16 +348,24 @@
     )(rows, cols, counts, feats, vals, dst, cot, w_self, w_neigh)
 
 
-def hand_kernel(out_h, w_h, source_h, out, w_self, w_neigh, source, sem):
+def hand_kernel(out_h, w_h, source_h, out, w_self, w_neigh, source, out_v, w_v, source_v, sem):
     half = w_self.shape[0]
-    pairs = (
-        (out_h, out), (w_h.at[pl.ds(0, half)], w_self), (w_h.at[pl.ds(half, half)], w_neigh), (source_h, source)
+    low, high = pl.ds(0, half), pl.ds(half, half)
+    ways = (
+        (w_h.at[low], w_v.at[low], w_self),
+        (w_h.at[high], w_v.at[high], w_neigh),
+        (out_h, out_v, out),
+        (source_h, source_v, source),
     )
-    copies = [pltpu.make_async_copy(src, dest, sem.at[i]) for i, (src, dest) in enumerate(pairs)]
-    for copy in copies:
-        copy.start()
-    for copy in copies:
-        copy.wait()
+    loads = [pltpu.make_async_copy(src, via, sem.at[0, i]) for i, (src, via, _) in enumerate(ways)]
+    stores = [pltpu.make_async_copy(via, dest, sem.at[1, i]) for i, (_, via, dest) in enumerate(ways)]
+    for load in loads:
+        load.start()
+    for load, store in zip(loads, stores):
+        load.wait()
+        store.start()
+    for store in stores:
+        store.wait()
 
 
 def hand(out, w_all, source):
@@ -371,7 +376,7 @@
         out_shape=(jax.ShapeDtypeStruct(out.shape, BF16), grad, grad, jax.ShapeDtypeStruct(source.shape, F32)),
         in_specs=[HBM] * 3,
         out_specs=(HBM,) * 4,
-        scratch_shapes=[DMA((4,))],
+        scratch_shapes=[*(pltpu.VMEM(a.shape, a.dtype) for a in (out, w_all, source)), DMA((2, 4))],
         compiler_params=pltpu.CompilerParams(vmem_limit_bytes=60 * 1024 * 1024),
     )(out, w_all, source)
 

time: 74.7 us -> 61.5 us (0.82)
  Pallas kernels: 73.2 us -> 60.1 us
    pallas_call x1, Pallas kernels: 13.1 us -> 1.73 us  [hand(): pl.pallas_call(hand_kernel, out_shape=(jax.ShapeDtypeStruct(out.shape, BF...]
    pallas_call x1, Pallas kernels: 60.2 us -> 58.3 us  [layer(): pl.pallas_call(functools.partial(layer_kernel, scale), out_shape=results,...]
where the time goes in v5:
time: 61.5 us; the launch traced here: 61.4 us
  Pallas kernels  60.1 us (98%)
  between operations  1.29 us (2%)
    pallas_call x1, Pallas kernels, layer(): pl.pallas_call(functools.partial(layer_kernel, scale), out_shape=results,...  58.3 us
    pallas_call x1, Pallas kernels, hand(): pl.pallas_call(hand_kernel, out_shape=(jax.ShapeDtypeStruct(out.shape, BF...  1.73 us

profile of v5, /device:TPU:1, one launch (start us, length us, event | category | flops | bytes accessed | tf_op | source)
XLA Modules:
  0.0 61.4 jit_solution(13939972425800812398)
XLA Ops:
  1.3 58.3 %shard_map.120 = (bf16[128,256]{1,0:T(8,128)(2,1)}, f32[32,8,256]{2,1,0:T(8,128)}, f32[128,128]{1,0:T(8,128)}) custom-call(s32[1,32]{1,0:T(1,128)} %bitcast.9, s32[1,32]{1,0:T(1,128)} %bitcast.10, s32[1,1]{1,0:T(1,128)S(6)} %copy.13.counts, bf16[16,128,128]{2,1,0:T(8,128)(2,1)} %bitcast.8, bf16[32,128,128]{2,1,0:T(8,128)(2,1)} %bitcast.7, ...), custom_call_target="tpu_custom_call" | custom-call | tf_op jit(solution)/shard_map/pallas_call | solution.py:325
  59.6 1.7 %shard_map.121 = (bf16[128,256]{1,0:T(8,128)(2,1)}, f32[16,8,256]{2,1,0:T(8,128)}, f32[16,8,256]{2,1,0:T(8,128)}, f32[128,128]{1,0:T(8,128)}) custom-call(bf16[128,256]{1,0:T(8,128)(2,1)} %get-tuple-element.11.out_h, f32[32,8,256]{2,1,0:T(8,128)} %get-tuple-element.12.w_h, f32[128,128]{1,0:T(8,128)} %get-tuple-element.13.source_h), custom_call_target="tpu_custom_call" | custom-call | tf_op jit(solution)/shard_map/pallas_call | solution.py:374

commit v6 on v5

--- a/solution.py
+++ b/solution.py
@@ -35,6 +35,7 @@
     def finish(self):
         for copy in self.started:
             copy.wait_send()
+        self.started = []
 
 
 def chain(ids, live):
@@ -52,10 +53,10 @@
 def layer_kernel(
     scale,
     rows_h, cols_h, counts, feats_h, vals_h, dst_h, cot_h, w_self_h, w_neigh_h,
-    out_h, w_out_h, source_h,
-    rows, cols, tables, table, out, w_out, source, feats, vals, dst, cot, w_self, w_neigh, sums, grads,
-    c_send, got_c, x_send, got_x, z_send, got_z,
-    h_send, got_h, y_send, got_y,
+    out_h, w_out_h, own_h, got_y,
+    rows, cols, tables, table, out, w_out, kept, feats, vals, dst, cot, w_self, w_neigh, sums, grads,
+    c_send, got_c, x_send, got_x, z_send, got_z, agg, pre_self, gpre,
+    h_send, got_h, y_send,
     w_full, w_c, w_half, w_send, got_w, w_mine, w_rows,
     load_sem, table_sem, store_sem,
     c_s, c_r, x_s, x_r, z_s, z_r, h_s, h_r, y_s, y_r,
@@ -68,6 +69,8 @@
     y, h = row // 2, row % 2
     slots = vals.shape[0]
     quarter = slots // 4
+    tall = dst.shape[0] // 2
+    halves = (pl.ds(0, tall), pl.ds(tall, tall))
 
     def at_col(zz, xx, kk):
         return (row, (zz % N) * 4 + xx * 2 + kk)
@@ -84,26 +87,6 @@
 
     def far(i):
         return at_row(y + i % N, (h + i // N) % 2)
-
-    barrier = pltpu.get_barrier_semaphore()
-
-    def wz_copy(i):
-        ref = w_send.at[((x + i // N) % 2) * N + (z + i) % N]
-        return remote(ref, got_w.at[i], wz_s.at[i], wz_r.at[i], near(i))
-
-    def wr_copy(i):
-        return remote(w_mine, w_rows.at[row], wr_s.at[i], wr_r.at[i], far(i))
-
-    def wg_copy(i):
-        return remote(w_out.at[me], w_out.at[me], wg_s.at[i], wg_r.at[i], near(i))
-
-    def greet(i, c):
-        pl.semaphore_signal(barrier, inc=1, device_id=near(i), device_id_type=MESH)
-        pl.semaphore_signal(barrier, inc=1, device_id=far(i), device_id_type=MESH)
-        return c
-
-    pl.semaphore_signal(barrier, inc=1, device_id=sibling, device_id_type=MESH)
-    lax.fori_loop(1, 2 * N, greet, 0)
 
     loads = []
     for i, (src, dest) in enumerate(((rows_h, rows), (cols_h, cols), (feats_h, feats))):
@@ -115,6 +98,26 @@
         loads.append(pltpu.make_async_copy(src, dest, load_sem.at[7 + i]))
     for load in loads:
         load.start()
+
+    barrier = pltpu.get_barrier_semaphore()
+
+    def wz_copy(i):
+        ref = w_send.at[((x + i // N) % 2) * N + (z + i) % N]
+        return remote(ref, got_w.at[i], wz_s.at[i], wz_r.at[i], near(i))
+
+    def wr_copy(i):
+        return remote(w_mine, w_rows.at[row], wr_s.at[i], wr_r.at[i], far(i))
+
+    def wg_copy(i):
+        return remote(w_out.at[me], w_out.at[me], wg_s.at[i], wg_r.at[i], near(i))
+
+    def greet(i, c):
+        pl.semaphore_signal(barrier, inc=1, device_id=near(i), device_id_type=MESH)
+        pl.semaphore_signal(barrier, inc=1, device_id=far(i), device_id_type=MESH)
+        return c
+
+    pl.semaphore_signal(barrier, inc=1, device_id=sibling, device_id_type=MESH)
+    lax.fori_loop(1, 2 * N, greet, 0)
 
     sums[slots] = jnp.zeros_like(sums[slots])
     tables[...] = jnp.zeros_like(tables)
@@ -144,90 +147,108 @@
     def c_copy(i):
         return remote(c_send.at[i], got_c.at[i], c_s.at[i], c_r.at[i], sibling)
 
-    for i in range(2 * N):
+    def c_step(i):
         c_send[i] = partial(z + OFFSETS[i % N], 1 - x if i < N else x, 1 - k).astype(BF16)
         remote.start(c_copy(i))
 
-    def x_copy(i):
-        return remote(x_send.at[i], got_x.at[i], x_s.at[i], x_r.at[i], beside)
+    for i in range(N):
+        c_step(i)
+
+    def x_copy(p, i):
+        return remote(
+            x_send.at[i, halves[p]], got_x.at[i, halves[p]], x_s.at[p, i], x_r.at[p, i], beside
+        )
 
     for i in range(N):
         own = partial(z + OFFSETS[i], 1 - x, k)
         c_copy(i).wait_recv()
         x_send[i] = (own + got_c[i].astype(F32)).astype(BF16)
-        remote.start(x_copy(i))
+        remote.start(x_copy(0, i))
+        c_step(N + i)
+    for i in range(N):
+        remote.start(x_copy(1, i))
 
     for load in loads[7:]:
         load.wait()
-    pre_self = jnp.dot(dst[...], w_self[...], preferred_element_type=F32)
-
-    def col_piece(i):
-        own = partial(z + OFFSETS[i], x, k)
-        c_copy(N + i).wait_recv()
-        own += got_c[N + i].astype(F32)
-        x_copy(i).wait_recv()
-        return own + got_x[i].astype(F32)
-
-    def z_copy(i):
-        return remote(z_send.at[i], got_z.at[i], z_s.at[i], z_r.at[i], at_col(z + OFFSETS[i], x, k))
-
-    for i in range(N - 1):
-        z_send[i] = col_piece(i).astype(BF16)
-        remote.start(z_copy(i))
-    total = col_piece(N - 1)
-    for i in range(N - 1):
-        z_copy(i).wait_recv()
-        total += got_z[i].astype(F32)
-    agg = total.astype(BF16)
-
-    pre = pre_self + jnp.dot(agg, w_neigh[...], preferred_element_type=F32)
-    sig = jax.nn.sigmoid(pre)
-    gpre = (cot[...].astype(F32) * sig * (1.0 + pre * (1.0 - sig))).astype(BF16)
-    grads[me] = lax.dot_general(
-        gpre, w_neigh[...], (((1,), (1,)), ((), ())), preferred_element_type=F32
-    ).astype(BF16)
-
-    def gz_copy(i):
-        ref = grads.at[me]
-        return remote(ref, ref, gz_s.at[i], gz_r.at[i], at_col(z + SPREAD[i], x, k))
-
-    def gx_copy(off):
-        ref = grads.at[mine + (z + N - off) % N]
-        return remote(ref, ref, gx_s.at[off], gx_r.at[off], beside)
+    pre_self[...] = jnp.dot(dst[...], w_self[...], preferred_element_type=F32)
+
+    def col_piece(p, i):
+        own = partial(z + OFFSETS[i], x, k)[p * tall : (p + 1) * tall]
+        if p == 0:
+            c_copy(N + i).wait_recv()
+        own += got_c[N + i, halves[p]].astype(F32)
+        x_copy(p, i).wait_recv()
+        return own + got_x[i, halves[p]].astype(F32)
+
+    def z_copy(p, i):
+        return remote(
+            z_send.at[i, halves[p]], got_z.at[i, halves[p]], z_s.at[p, i], z_r.at[p, i], at_col(z + OFFSETS[i], x, k)
+        )
+
+    def gz_copy(p, i):
+        ref = grads.at[me, halves[p]]
+        return remote(ref, ref, gz_s.at[p, i], gz_r.at[p, i], at_col(z + SPREAD[i], x, k))
+
+    def gx_copy(p, off):
+        ref = grads.at[mine + (z + N - off) % N, halves[p]]
+        return remote(ref, ref, gx_s.at[p, off], gx_r.at[p, off], beside)
 
     def gc_copy(other, off):
         ref = grads.at[k * 2 * N + ((x + other) % 2) * N + (z + N - off) % N]
         return remote(ref, ref, gc_s.at[other * N + off], gc_r.at[other * N + off], sibling)
 
-    for i in range(N - 1):
-        remote.start(gz_copy(i))
-    remote.start(gx_copy(0))
+    totals = []
+    for p in range(2):
+        for i in range(N - 1):
+            z_send[i, halves[p]] = col_piece(p, i).astype(BF16)
+            remote.start(z_copy(p, i))
+        totals.append(col_piece(p, N - 1))
+
+    for p, rows_p in enumerate(halves):
+        total = totals[p]
+        for i in range(N - 1):
+            z_copy(p, i).wait_recv()
+            total += got_z[i, rows_p].astype(F32)
+        agg[rows_p] = total.astype(BF16)
+        pre = pre_self[rows_p] + jnp.dot(agg[rows_p], w_neigh[...], preferred_element_type=F32)
+        sig = jax.nn.sigmoid(pre)
+        gpre[rows_p] = (cot[rows_p].astype(F32) * sig * (1.0 + pre * (1.0 - sig))).astype(BF16)
+        grads[me, rows_p] = lax.dot_general(
+            gpre[rows_p], w_neigh[...], (((1,), (1,)), ((), ())), preferred_element_type=F32
+        ).astype(BF16)
+        for i in range(N - 1):
+            remote.start(gz_copy(p, i))
+        remote.start(gx_copy(p, 0))
+        out[rows_p] = (pre * sig).astype(BF16)
     remote.start(gc_copy(0, 0))
-    out[...] = (pre * sig).astype(BF16)
     stores = [pltpu.make_async_copy(out, out_h, store_sem.at[0])]
     stores[0].start()
 
     feat = dst.shape[1]
     pieces, wide, hid = w_full.shape
     half = pieces // 2
-    for base, left in ((0, dst[...]), (1, agg)):
-        dw = lax.dot_general(left, gpre, (((0,), (0,)), ((), ())), preferred_element_type=F32)
+    for base, left in ((0, dst), (1, agg)):
+        dw = lax.dot_general(left[...], gpre[...], (((0,), (0,)), ((), ())), preferred_element_type=F32)
         w_full[pl.ds(base * half, half)] = dw.reshape(half, wide, hid)
     wc_copy = remote(w_full.at[pl.ds((1 - k) * half, half)], w_c, wc_s, wc_r, sibling)
     remote.start(wc_copy)
 
     def from_beside(off):
-        gx_copy(off).wait_recv()
+        gx_copy(0, off).wait_recv()
+        gx_copy(1, off).wait_recv()
         remote.start(gc_copy(1, off))
 
+    for i, off in enumerate(SPREAD):
+        gz_copy(0, i).wait_recv()
+        remote.start(gx_copy(0, off))
     wc_copy.wait_recv()
     w_half[...] = w_full[pl.ds(k * half, half)] + w_c[...]
     w_send[...] = w_half[...].astype(BF16)
     for i in range(1, 2 * N):
         remote.start(wz_copy(i))
     for i, off in enumerate(SPREAD):
-        gz_copy(i).wait_recv()
-        remote.start(gx_copy(off))
+        gz_copy(1, i).wait_recv()
+        remote.start(gx_copy(1, off))
         remote.start(gc_copy(0, off))
         if i == 3:
             from_beside(0)
@@ -281,25 +302,22 @@
         y_send[i] = row_piece(i).astype(BF16)
         remote.start(y_copy(i))
 
+    kept[...] = row_piece(N - 1)
+    stores.append(pltpu.make_async_copy(kept, own_h, store_sem.at[1]))
+    stores[1].start()
     for i in range(1, 2 * N):
         wg_copy(i).wait_recv()
-    ref = w_out.at[pl.ds(k * half, half)]
-    wl_copy = remote(ref, ref, wl_s, wl_r, sibling)
+    ref = pl.ds(k * half, half)
+    wl_copy = remote(w_out.at[ref], w_out_h.at[ref], wl_s, wl_r, sibling)
     remote.start(wl_copy)
-
-    total = row_piece(N - 1)
-    for i in range(N - 1):
-        y_copy(i).wait_recv()
-        total += got_y[i].astype(F32)
-    source[...] = total
-    stores.append(pltpu.make_async_copy(source, source_h, store_sem.at[1]))
-    stores[1].start()
-    wl_copy.wait_recv()
-    stores.append(pltpu.make_async_copy(w_out, w_out_h, store_sem.at[2]))
+    stores.append(pltpu.make_async_copy(w_out.at[ref], w_out_h.at[ref], store_sem.at[2]))
     stores[2].start()
     remote.finish()
     for store in stores:
         store.wait()
+    for i in range(N - 1):
+        y_copy(i).wait_recv()
+    wl_copy.wait_recv()
 
 
 def layer(scale, rows, cols, counts, feats, vals, dst, cot, w_self, w_neigh):
@@ -311,6 +329,7 @@
         jax.ShapeDtypeStruct((block, hid), BF16),
         jax.ShapeDtypeStruct((4 * N, wide, hid), F32),
         jax.ShapeDtypeStruct((block, width), F32),
+        jax.ShapeDtypeStruct((N - 1, block, width), BF16),
     )
 
     def like(a):
@@ -326,19 +345,20 @@
         functools.partial(layer_kernel, scale),
         out_shape=results,
         in_specs=[HBM, HBM, SMEM] + [HBM] * 6,
-        out_specs=(HBM,) * 3,
+        out_specs=(HBM,) * 4,
         scratch_shapes=[
             like(rows), like(cols), pltpu.VMEM((8, 128), jnp.int32), pltpu.SMEM((8, 128), jnp.int32),
-            *map(like, results), like(feats), like(vals), like(dst), like(cot), like(w_self), like(w_neigh),
+            *map(like, results[:3]), like(feats), like(vals), like(dst), like(cot), like(w_self), like(w_neigh),
             blocks(slots + 1, F32), blocks(4 * N),
             blocks(2 * N), blocks(2 * N), blocks(N), blocks(N), blocks(N - 1), blocks(N - 1),
-            blocks(N), blocks(N), blocks(N - 1), blocks(N - 1),
+            like(dst), pltpu.VMEM(cot.shape, F32), like(cot),
+            blocks(N), blocks(N), blocks(N - 1),
             slabs(4 * N), slabs(2 * N), slabs(2 * N), slabs(2 * N, BF16), slabs(2 * N, BF16),
             pltpu.VMEM((wide, hid), F32), slabs(2 * N),
             DMA((11,)), DMA, DMA((3,)),
-            DMA((2 * N,)), DMA((2 * N,)), DMA((N,)), DMA((N,)), DMA((N,)), DMA((N,)),
+            DMA((2 * N,)), DMA((2 * N,)), DMA((2, N)), DMA((2, N)), DMA((2, N)), DMA((2, N)),
             DMA((N,)), DMA((N,)), DMA((N,)), DMA((N,)),
-            DMA((N,)), DMA((N,)), DMA((N,)), DMA((N,)), DMA((2 * N,)), DMA((2 * N,)),
+            DMA((2, N)), DMA((2, N)), DMA((2, N)), DMA((2, N)), DMA((2 * N,)), DMA((2 * N,)),
             DMA, DMA, DMA((2 * N,)), DMA((2 * N,)), DMA((2 * N,)), DMA((2 * N,)), DMA((2 * N,)), DMA((2 * N,)),
             DMA, DMA,
         ],
@@ -348,37 +368,45 @@
     )(rows, cols, counts, feats, vals, dst, cot, w_self, w_neigh)
 
 
-def hand_kernel(out_h, w_h, source_h, out, w_self, w_neigh, source, out_v, w_v, source_v, sem):
+def hand_kernel(out_h, w_h, own_h, parts_h, out, w_self, w_neigh, source, out_v, w_v, own_v, parts_v, sem):
     half = w_self.shape[0]
     low, high = pl.ds(0, half), pl.ds(half, half)
     ways = (
+        (parts_h, parts_v, None),
+        (own_h, own_v, source),
         (w_h.at[low], w_v.at[low], w_self),
         (w_h.at[high], w_v.at[high], w_neigh),
         (out_h, out_v, out),
-        (source_h, source_v, source),
     )
     loads = [pltpu.make_async_copy(src, via, sem.at[0, i]) for i, (src, via, _) in enumerate(ways)]
-    stores = [pltpu.make_async_copy(via, dest, sem.at[1, i]) for i, (_, via, dest) in enumerate(ways)]
+    stores = [pltpu.make_async_copy(via, dest, sem.at[1, i]) for i, (_, via, dest) in enumerate(ways) if dest is not None]
     for load in loads:
         load.start()
-    for load, store in zip(loads, stores):
+    for load in loads[:2]:
+        load.wait()
+    total = own_v[...]
+    for i in range(parts_v.shape[0]):
+        total += parts_v[i].astype(F32)
+    own_v[...] = total
+    stores[0].start()
+    for load, store in zip(loads[2:], stores[1:]):
         load.wait()
         store.start()
     for store in stores:
         store.wait()
 
 
-def hand(out, w_all, source):
+def hand(out, w_all, own, parts):
     pieces, wide, hid = w_all.shape
     grad = jax.ShapeDtypeStruct((pieces // 2, wide, hid), F32)
     return pl.pallas_call(
         hand_kernel,
-        out_shape=(jax.ShapeDtypeStruct(out.shape, BF16), grad, grad, jax.ShapeDtypeStruct(source.shape, F32)),
-        in_specs=[HBM] * 3,
+        out_shape=(jax.ShapeDtypeStruct(out.shape, BF16), grad, grad, jax.ShapeDtypeStruct(own.shape, F32)),
+        in_specs=[HBM] * 4,
         out_specs=(HBM,) * 4,
-        scratch_shapes=[*(pltpu.VMEM(a.shape, a.dtype) for a in (out, w_all, source)), DMA((2, 4))],
+        scratch_shapes=[*(pltpu.VMEM(a.shape, a.dtype) for a in (out, w_all, own, parts)), DMA((2, 5))],
         compiler_params=pltpu.CompilerParams(vmem_limit_bytes=60 * 1024 * 1024),
-    )(out, w_all, source)
+    )(out, w_all, own, parts)
 
 
 def per_device(features, dst_features, w_self, w_neigh, cotangent, block_values, block_rows, block_cols, block_counts):

time: 61.5 us -> 59.2 us (0.963)
  Pallas kernels: 60.1 us -> 57.8 us
    pallas_call x1, Pallas kernels: 58.3 us -> 55.9 us  [layer(): pl.pallas_call(functools.partial(layer_kernel, scale), out_shape=results,...]
where the time goes in v6:
time: 59.2 us; the launch traced here: 59 us
  Pallas kernels  57.8 us (98%)
  between operations  1.29 us (2%)
    pallas_call x1, Pallas kernels, layer(): pl.pallas_call(functools.partial(layer_kernel, scale), out_shape=results,...  55.9 us
    pallas_call x1, Pallas kernels, hand(): pl.pallas_call(hand_kernel, out_shape=(jax.ShapeDtypeStruct(out.shape, BF...  1.87 us

profile of v6, /device:TPU:1, one launch (start us, length us, event | category | flops | bytes accessed | tf_op | source)
XLA Modules:
  0.0 59.0 jit_solution(10872198829321471204)
XLA Ops:
  1.3 55.9 %shard_map.120 = (bf16[128,256]{1,0:T(8,128)(2,1)}, f32[32,8,256]{2,1,0:T(8,128)}, f32[128,128]{1,0:T(8,128)}, bf16[7,128,128]{2,1,0:T(8,128)(2,1)}) custom-call(s32[1,32]{1,0:T(1,128)} %bitcast.9, s32[1,32]{1,0:T(1,128)} %bitcast.10, s32[1,1]{1,0:T(1,128)S(6)} %copy.13.counts, bf16[16,128,128]{2,1,0:T(8,128)(2,1)} %bitcast.8, ...), custom_call_target="tpu_custom_call" | custom-call | tf_op jit(solution)/shard_map/pallas_call | solution.py:344
  57.2 1.9 %shard_map.121 = (bf16[128,256]{1,0:T(8,128)(2,1)}, f32[16,8,256]{2,1,0:T(8,128)}, f32[16,8,256]{2,1,0:T(8,128)}, f32[128,128]{1,0:T(8,128)}) custom-call(bf16[128,256]{1,0:T(8,128)(2,1)} %get-tuple-element.12.out_h, f32[32,8,256]{2,1,0:T(8,128)} %get-tuple-element.13.w_h, f32[128,128]{1,0:T(8,128)} %get-tuple-element.14.own_h, ...), custom_call_target="tpu_custom_call" | custom-call | tf_op jit(solution)/shard_map/pallas_call | solution.py:402

commit v7 on v6

--- a/solution.py
+++ b/solution.py
@@ -12,7 +12,10 @@
 F32 = jnp.float32
 MESH = pl.DeviceIdType.MESH
 N = 8
+SHARES = (64, 64)
+PARTS = len(SHARES)
 OFFSETS = (4, 3, 5, 2, 6, 1, 7, 0)
+GREETED = (12, 4, 11, 13, 3, 5, 10, 14, 2, 6, 9, 15, 1, 7, 8)
 SPREAD = (1, 7, 2, 6, 3, 5, 4)
 SMEM = pl.BlockSpec(memory_space=pltpu.SMEM)
 HBM = pl.BlockSpec(memory_space=pltpu.HBM)
@@ -69,8 +72,7 @@
     y, h = row // 2, row % 2
     slots = vals.shape[0]
     quarter = slots // 4
-    tall = dst.shape[0] // 2
-    halves = (pl.ds(0, tall), pl.ds(tall, tall))
+    shares = [pl.ds(sum(SHARES[:p]), tall) for p, tall in enumerate(SHARES)]
 
     def at_col(zz, xx, kk):
         return (row, (zz % N) * 4 + xx * 2 + kk)
@@ -87,6 +89,26 @@
 
     def far(i):
         return at_row(y + i % N, (h + i // N) % 2)
+
+    def wz_copy(i):
+        ref = w_send.at[((x + i // N) % 2) * N + (z + i) % N]
+        return remote(ref, got_w.at[i], wz_s.at[i], wz_r.at[i], near(i))
+
+    def wr_copy(i):
+        return remote(w_mine, w_rows.at[row], wr_s.at[i], wr_r.at[i], far(i))
+
+    def wg_copy(i):
+        return remote(w_out.at[me], w_out.at[me], wg_s.at[i], wg_r.at[i], near(i))
+
+    barrier = pltpu.get_barrier_semaphore()
+
+    def greet(device):
+        pl.semaphore_signal(barrier, inc=1, device_id=device, device_id_type=MESH)
+
+    for i in GREETED:
+        greet(far(i))
+        greet(near(i))
+    greet(sibling)
 
     loads = []
     for i, (src, dest) in enumerate(((rows_h, rows), (cols_h, cols), (feats_h, feats))):
@@ -98,26 +120,6 @@
         loads.append(pltpu.make_async_copy(src, dest, load_sem.at[7 + i]))
     for load in loads:
         load.start()
-
-    barrier = pltpu.get_barrier_semaphore()
-
-    def wz_copy(i):
-        ref = w_send.at[((x + i // N) % 2) * N + (z + i) % N]
-        return remote(ref, got_w.at[i], wz_s.at[i], wz_r.at[i], near(i))
-
-    def wr_copy(i):
-        return remote(w_mine, w_rows.at[row], wr_s.at[i], wr_r.at[i], far(i))
-
-    def wg_copy(i):
-        return remote(w_out.at[me], w_out.at[me], wg_s.at[i], wg_r.at[i], near(i))
-
-    def greet(i, c):
-        pl.semaphore_signal(barrier, inc=1, device_id=near(i), device_id_type=MESH)
-        pl.semaphore_signal(barrier, inc=1, device_id=far(i), device_id_type=MESH)
-        return c
-
-    pl.semaphore_signal(barrier, inc=1, device_id=sibling, device_id_type=MESH)
-    lax.fori_loop(1, 2 * N, greet, 0)
 
     sums[slots] = jnp.zeros_like(sums[slots])
     tables[...] = jnp.zeros_like(tables)
@@ -156,7 +158,7 @@
 
     def x_copy(p, i):
         return remote(
-            x_send.at[i, halves[p]], got_x.at[i, halves[p]], x_s.at[p, i], x_r.at[p, i], beside
+            x_send.at[i, shares[p]], got_x.at[i, shares[p]], x_s.at[p, i], x_r.at[p, i], beside
         )
 
     for i in range(N):
@@ -165,32 +167,34 @@
         x_send[i] = (own + got_c[i].astype(F32)).astype(BF16)
         remote.start(x_copy(0, i))
         c_step(N + i)
-    for i in range(N):
-        remote.start(x_copy(1, i))
+    for p in range(1, PARTS):
+        for i in range(N):
+            remote.start(x_copy(p, i))
 
     for load in loads[7:]:
         load.wait()
     pre_self[...] = jnp.dot(dst[...], w_self[...], preferred_element_type=F32)
 
     def col_piece(p, i):
-        own = partial(z + OFFSETS[i], x, k)[p * tall : (p + 1) * tall]
+        first = sum(SHARES[:p])
+        own = partial(z + OFFSETS[i], x, k)[first : first + SHARES[p]]
         if p == 0:
             c_copy(N + i).wait_recv()
-        own += got_c[N + i, halves[p]].astype(F32)
+        own += got_c[N + i, shares[p]].astype(F32)
         x_copy(p, i).wait_recv()
-        return own + got_x[i, halves[p]].astype(F32)
+        return own + got_x[i, shares[p]].astype(F32)
 
     def z_copy(p, i):
         return remote(
-            z_send.at[i, halves[p]], got_z.at[i, halves[p]], z_s.at[p, i], z_r.at[p, i], at_col(z + OFFSETS[i], x, k)
+            z_send.at[i, shares[p]], got_z.at[i, shares[p]], z_s.at[p, i], z_r.at[p, i], at_col(z + OFFSETS[i], x, k)
         )
 
     def gz_copy(p, i):
-        ref = grads.at[me, halves[p]]
+        ref = grads.at[me, shares[p]]
         return remote(ref, ref, gz_s.at[p, i], gz_r.at[p, i], at_col(z + SPREAD[i], x, k))
 
     def gx_copy(p, off):
-        ref = grads.at[mine + (z + N - off) % N, halves[p]]
+        ref = grads.at[mine + (z + N - off) % N, shares[p]]
         return remote(ref, ref, gx_s.at[p, off], gx_r.at[p, off], beside)
 
     def gc_copy(other, off):
@@ -198,13 +202,13 @@
         return remote(ref, ref, gc_s.at[other * N + off], gc_r.at[other * N + off], sibling)
 
     totals = []
-    for p in range(2):
+    for p in range(PARTS):
         for i in range(N - 1):
-            z_send[i, halves[p]] = col_piece(p, i).astype(BF16)
+            z_send[i, shares[p]] = col_piece(p, i).astype(BF16)
             remote.start(z_copy(p, i))
         totals.append(col_piece(p, N - 1))
 
-    for p, rows_p in enumerate(halves):
+    for p, rows_p in enumerate(shares):
         total = totals[p]
         for i in range(N - 1):
             z_copy(p, i).wait_recv()
@@ -234,21 +238,22 @@
     remote.start(wc_copy)
 
     def from_beside(off):
-        gx_copy(0, off).wait_recv()
-        gx_copy(1, off).wait_recv()
+        for p in range(PARTS):
+            gx_copy(p, off).wait_recv()
         remote.start(gc_copy(1, off))
 
-    for i, off in enumerate(SPREAD):
-        gz_copy(0, i).wait_recv()
-        remote.start(gx_copy(0, off))
+    for p in range(PARTS - 1):
+        for i, off in enumerate(SPREAD):
+            gz_copy(p, i).wait_recv()
+            remote.start(gx_copy(p, off))
     wc_copy.wait_recv()
     w_half[...] = w_full[pl.ds(k * half, half)] + w_c[...]
     w_send[...] = w_half[...].astype(BF16)
     for i in range(1, 2 * N):
         remote.start(wz_copy(i))
     for i, off in enumerate(SPREAD):
-        gz_copy(1, i).wait_recv()
-        remote.start(gx_copy(1, off))
+        gz_copy(PARTS - 1, i).wait_recv()
+        remote.start(gx_copy(PARTS - 1, off))
         remote.start(gc_copy(0, off))
         if i == 3:
             from_beside(0)
@@ -356,9 +361,9 @@
             slabs(4 * N), slabs(2 * N), slabs(2 * N), slabs(2 * N, BF16), slabs(2 * N, BF16),
             pltpu.VMEM((wide, hid), F32), slabs(2 * N),
             DMA((11,)), DMA, DMA((3,)),
-            DMA((2 * N,)), DMA((2 * N,)), DMA((2, N)), DMA((2, N)), DMA((2, N)), DMA((2, N)),
+            DMA((2 * N,)), DMA((2 * N,)), DMA((PARTS, N)), DMA((PARTS, N)), DMA((PARTS, N)), DMA((PARTS, N)),
             DMA((N,)), DMA((N,)), DMA((N,)), DMA((N,)),
-            DMA((2, N)), DMA((2, N)), DMA((2, N)), DMA((2, N)), DMA((2 * N,)), DMA((2 * N,)),
+            DMA((PARTS, N)), DMA((PARTS, N)), DMA((PARTS, N)), DMA((PARTS, N)), DMA((2 * N,)), DMA((2 * N,)),
             DMA, DMA, DMA((2 * N,)), DMA((2 * N,)), DMA((2 * N,)), DMA((2 * N,)), DMA((2 * N,)), DMA((2 * N,)),
             DMA, DMA,
         ],

time: 59.2 us -> 58.6 us (0.990)
  Pallas kernels: 57.8 us -> 57.2 us
    pallas_call x1, Pallas kernels: 55.9 us -> 55.3 us  [layer(): pl.pallas_call(functools.partial(layer_kernel, scale), out_shape=results,...]
where the time goes in v7:
time: 58.6 us; the launch traced here: 58.4 us
  Pallas kernels  57.2 us (98%)
  between operations  1.29 us (2%)
    pallas_call x1, Pallas kernels, layer(): pl.pallas_call(functools.partial(layer_kernel, scale), out_shape=results,...  55.3 us
    pallas_call x1, Pallas kernels, hand(): pl.pallas_call(hand_kernel, out_shape=(jax.ShapeDtypeStruct(out.shape, BF...  1.87 us

profile of v7, /device:TPU:1, one launch (start us, length us, event | category | flops | bytes accessed | tf_op | source)
XLA Modules:
  0.0 58.4 jit_solution(7626719056019364323)
XLA Ops:
  1.3 55.3 %shard_map.120 = (bf16[128,256]{1,0:T(8,128)(2,1)}, f32[32,8,256]{2,1,0:T(8,128)}, f32[128,128]{1,0:T(8,128)}, bf16[7,128,128]{2,1,0:T(8,128)(2,1)}) custom-call(s32[1,32]{1,0:T(1,128)} %bitcast.9, s32[1,32]{1,0:T(1,128)} %bitcast.10, s32[1,1]{1,0:T(1,128)S(6)} %copy.13.counts, bf16[16,128,128]{2,1,0:T(8,128)(2,1)} %bitcast.8, ...), custom_call_target="tpu_custom_call" | custom-call | tf_op jit(solution)/shard_map/pallas_call | solution.py:349
  56.6 1.9 %shard_map.121 = (bf16[128,256]{1,0:T(8,128)(2,1)}, f32[16,8,256]{2,1,0:T(8,128)}, f32[16,8,256]{2,1,0:T(8,128)}, f32[128,128]{1,0:T(8,128)}) custom-call(bf16[128,256]{1,0:T(8,128)(2,1)} %get-tuple-element.12.out_h, f32[32,8,256]{2,1,0:T(8,128)} %get-tuple-element.13.w_h, f32[128,128]{1,0:T(8,128)} %get-tuple-element.14.own_h, ...), custom_call_target="tpu_custom_call" | custom-call | tf_op jit(solution)/shard_map/pallas_call | solution.py:407

commit v8 on v7

--- a/solution.py
+++ b/solution.py
@@ -16,7 +16,7 @@
 PARTS = len(SHARES)
 OFFSETS = (4, 3, 5, 2, 6, 1, 7, 0)
 GREETED = (12, 4, 11, 13, 3, 5, 10, 14, 2, 6, 9, 15, 1, 7, 8)
-SPREAD = (1, 7, 2, 6, 3, 5, 4)
+SPREAD = (4, 3, 5, 2, 6, 1, 7)
 SMEM = pl.BlockSpec(memory_space=pltpu.SMEM)
 HBM = pl.BlockSpec(memory_space=pltpu.HBM)
 DMA = pltpu.SemaphoreType.DMA
@@ -144,17 +144,18 @@
     def partial(zz, xx, kk):
         return sums[table[1, (zz % N) * 4 + xx * 2 + kk]]
 
+    for i in range(2 * N):
+        c_send[i] = partial(z + OFFSETS[i % N], 1 - x if i < N else x, 1 - k).astype(BF16)
+    for load in loads[7:]:
+        load.wait()
+    pre_self[...] = jnp.dot(dst[...], w_self[...], preferred_element_type=F32)
     pl.semaphore_wait(barrier, 4 * N - 1)
 
     def c_copy(i):
         return remote(c_send.at[i], got_c.at[i], c_s.at[i], c_r.at[i], sibling)
 
-    def c_step(i):
-        c_send[i] = partial(z + OFFSETS[i % N], 1 - x if i < N else x, 1 - k).astype(BF16)
+    for i in range(N):
         remote.start(c_copy(i))
-
-    for i in range(N):
-        c_step(i)
 
     def x_copy(p, i):
         return remote(
@@ -166,14 +167,10 @@
         c_copy(i).wait_recv()
         x_send[i] = (own + got_c[i].astype(F32)).astype(BF16)
         remote.start(x_copy(0, i))
-        c_step(N + i)
+        remote.start(c_copy(N + i))
     for p in range(1, PARTS):
         for i in range(N):
             remote.start(x_copy(p, i))
-
-    for load in loads[7:]:
-        load.wait()
-    pre_self[...] = jnp.dot(dst[...], w_self[...], preferred_element_type=F32)
 
     def col_piece(p, i):
         first = sum(SHARES[:p])

time: 58.6 us -> 57.6 us (0.983)
  Pallas kernels: 57.2 us -> 56.2 us
    pallas_call x1, Pallas kernels: 55.3 us -> 54.3 us  [layer(): pl.pallas_call(functools.partial(layer_kernel, scale), out_shape=results,...]
where the time goes in v8:
time: 57.6 us; the launch traced here: 57.5 us
  Pallas kernels  56.2 us (98%)
  between operations  1.29 us (2%)
    pallas_call x1, Pallas kernels, layer(): pl.pallas_call(functools.partial(layer_kernel, scale), out_shape=results,...  54.3 us
    pallas_call x1, Pallas kernels, hand(): pl.pallas_call(hand_kernel, out_shape=(jax.ShapeDtypeStruct(out.shape, BF...  1.87 us

profile of v8, /device:TPU:1, one launch (start us, length us, event | category | flops | bytes accessed | tf_op | source)
XLA Modules:
  0.0 57.5 jit_solution(12992561728420896418)
XLA Ops:
  1.3 54.3 %shard_map.120 = (bf16[128,256]{1,0:T(8,128)(2,1)}, f32[32,8,256]{2,1,0:T(8,128)}, f32[128,128]{1,0:T(8,128)}, bf16[7,128,128]{2,1,0:T(8,128)(2,1)}) custom-call(s32[1,32]{1,0:T(1,128)} %bitcast.9, s32[1,32]{1,0:T(1,128)} %bitcast.10, s32[1,1]{1,0:T(1,128)S(6)} %copy.13.counts, bf16[16,128,128]{2,1,0:T(8,128)(2,1)} %bitcast.8, ...), custom_call_target="tpu_custom_call" | custom-call | tf_op jit(solution)/shard_map/pallas_call | solution.py:346
  55.6 1.9 %shard_map.121 = (bf16[128,256]{1,0:T(8,128)(2,1)}, f32[16,8,256]{2,1,0:T(8,128)}, f32[16,8,256]{2,1,0:T(8,128)}, f32[128,128]{1,0:T(8,128)}) custom-call(bf16[128,256]{1,0:T(8,128)(2,1)} %get-tuple-element.12.out_h, f32[32,8,256]{2,1,0:T(8,128)} %get-tuple-element.13.w_h, f32[128,128]{1,0:T(8,128)} %get-tuple-element.14.own_h, ...), custom_call_target="tpu_custom_call" | custom-call | tf_op jit(solution)/shard_map/pallas_call | solution.py:404

commit v9 on v8

--- a/solution.py
+++ b/solution.py
@@ -252,8 +252,6 @@
         gz_copy(PARTS - 1, i).wait_recv()
         remote.start(gx_copy(PARTS - 1, off))
         remote.start(gc_copy(0, off))
-        if i == 3:
-            from_beside(0)
 
     total = w_half[x * N + z]
     for i in range(1, 2 * N):
@@ -263,7 +261,7 @@
     w_rows[row] = total
     for i in range(1, 2 * N):
         remote.start(wr_copy(i))
-    for off in SPREAD:
+    for off in (0, *SPREAD):
         from_beside(off)
     for i in range(2 * N):
         gc_copy(i // N, i % N).wait_recv()
@@ -283,15 +281,6 @@
         h_send[i] = source_partial(y + OFFSETS[i], 1 - h).astype(BF16)
         remote.start(h_copy(i))
 
-    for i in range(1, 2 * N):
-        wr_copy(i).wait_recv()
-    total = w_rows[0]
-    for i in range(1, 2 * N):
-        total += w_rows[i]
-    w_out[me] = total * scale
-    for i in range(1, 2 * N):
-        remote.start(wg_copy(i))
-
     def y_copy(i):
         return remote(y_send.at[i], got_y.at[i], y_s.at[i], y_r.at[i], at_row(y + OFFSETS[i], h))
 
@@ -300,7 +289,19 @@
         h_copy(i).wait_recv()
         return own + got_h[i].astype(F32)
 
+    def row_sum():
+        for i in range(1, 2 * N):
+            wr_copy(i).wait_recv()
+        total = w_rows[0]
+        for i in range(1, 2 * N):
+            total += w_rows[i]
+        w_out[me] = total * scale
+        for i in range(1, 2 * N):
+            remote.start(wg_copy(i))
+
     for i in range(N - 1):
+        if i == 2:
+            row_sum()
         y_send[i] = row_piece(i).astype(BF16)
         remote.start(y_copy(i))
 

time: 57.6 us -> 58.4 us (1.014)
  Pallas kernels: 56.2 us -> 56.9 us
    pallas_call x1, Pallas kernels: 54.3 us -> 55 us  [layer(): pl.pallas_call(functools.partial(layer_kernel, scale), out_shape=results,...]
where the time goes in v9:
time: 58.4 us; the launch traced here: 58.2 us
  Pallas kernels  56.9 us (97%)
  between operations  1.29 us (2%)
    pallas_call x1, Pallas kernels, layer(): pl.pallas_call(functools.partial(layer_kernel, scale), out_shape=results,...  55 us
    pallas_call x1, Pallas kernels, hand(): pl.pallas_call(hand_kernel, out_shape=(jax.ShapeDtypeStruct(out.shape, BF...  1.87 us

profile of v9, /device:TPU:1, one launch (start us, length us, event | category | flops | bytes accessed | tf_op | source)
XLA Modules:
  0.0 58.2 jit_solution(11726119539953746405)
XLA Ops:
  1.3 55.0 %shard_map.120 = (bf16[128,256]{1,0:T(8,128)(2,1)}, f32[32,8,256]{2,1,0:T(8,128)}, f32[128,128]{1,0:T(8,128)}, bf16[7,128,128]{2,1,0:T(8,128)(2,1)}) custom-call(s32[1,32]{1,0:T(1,128)} %bitcast.9, s32[1,32]{1,0:T(1,128)} %bitcast.10, s32[1,1]{1,0:T(1,128)S(6)} %copy.13.counts, bf16[16,128,128]{2,1,0:T(8,128)(2,1)} %bitcast.8, ...), custom_call_target="tpu_custom_call" | custom-call | tf_op jit(solution)/shard_map/pallas_call | solution.py:347
  56.3 1.9 %shard_map.121 = (bf16[128,256]{1,0:T(8,128)(2,1)}, f32[16,8,256]{2,1,0:T(8,128)}, f32[16,8,256]{2,1,0:T(8,128)}, f32[128,128]{1,0:T(8,128)}) custom-call(bf16[128,256]{1,0:T(8,128)(2,1)} %get-tuple-element.12.out_h, f32[32,8,256]{2,1,0:T(8,128)} %get-tuple-element.13.w_h, f32[128,128]{1,0:T(8,128)} %get-tuple-element.14.own_h, ...), custom_call_target="tpu_custom_call" | custom-call | tf_op jit(solution)/shard_map/pallas_call | solution.py:405
